TPU v7x, 32 devices: a whole 2x2x4 slice. The times are simulated.
32 devices in a mesh: dp: 8 (over z, x), row: 2 (over core), col: 2 (over y).
Axes of the slice: x: 2, y: 2, z: 4, core: 2. Of those that a mesh axis runs over, the one named last changes fastest.
Arguments:
- tokens: bfloat16 [2, 8, 256, 2048], P(None, None, 'dp', ('row', 'col')), may hold values from -57 to 57
- lengths: int32 [2, 8], replicated, may hold values from 64 to 256, as said below
- deal_order: int32 [2, 8], replicated, may hold values from 0 to 7, each once within a row
- attention_gain: float32 [2048], P(('row', 'col')), may hold values from 0.25 to 1.75
- query_weight: bfloat16 [2048, 2048], P('row', 'col'), may hold values from -0.1875 to 0.1875
- key_weight: bfloat16 [2048, 2048], P('row', 'col'), may hold values from -0.1875 to 0.1875
- value_weight: bfloat16 [2048, 2048], P('row', 'col'), may hold values from -0.125 to 0.125
- output_weight: bfloat16 [2048, 2048], P('col', 'row'), may hold values from -0.25 to 0.25
- feed_gain: float32 [2048], P(('row', 'col')), may hold values from 0.25 to 1.75
- gate_weight: bfloat16 [2048, 8192], P('row', 'col'), may hold values from -0.125 to 0.125
- up_weight: bfloat16 [2048, 8192], P('row', 'col'), may hold values from -0.125 to 0.125
- down_weight: bfloat16 [8192, 2048], P('col', 'row'), may hold values from -0.09375 to 0.09375
- cotangent: bfloat16 [2, 8, 256, 2048], P(None, 'dp', None, ('row', 'col')), may hold values from -6 to 6
Outputs:
- layer_output: bfloat16 [2, 8, 256, 2048], P(None, None, 'dp', ('row', 'col'))
- tokens_grad: bfloat16 [2, 8, 256, 2048], P(None, None, 'dp', ('row', 'col'))
- attention_gain_grad: float32 [2048], P(('row', 'col', 'dp'))
- query_grad: float32 [2048, 2048], P(('row', 'dp'), 'col')
- key_grad: float32 [2048, 2048], P(('row', 'dp'), 'col')
- value_grad: float32 [2048, 2048], P(('row', 'dp'), 'col')
- output_grad: float32 [2048, 2048], P(('col', 'dp'), 'row')
- feed_gain_grad: float32 [2048], P(('row', 'col', 'dp'))
- gate_grad: float32 [2048, 8192], P(('row', 'dp'), 'col')
- up_grad: float32 [2048, 8192], P(('row', 'dp'), 'col')
- down_grad: float32 [8192, 2048], P(('col', 'dp'), 'row')
Inputs may be any that keep to these rules, and one draw needn't show every extreme that they name: `lengths`: in each micro-batch one sequence has exactly 256 tokens. `deal_order`: each row holds every number of 0 to 7 once.
All inputs are finite; a program needn't handle non-finite values.
Results may differ from a plain program's by a relative error of at most 0.023.
Values may be sent and summed in bfloat16 or wider, within the bound.
A program may use at most 256 MiB of HBM per device.

v0:
```python
import math

import jax
import jax.numpy as jnp
from jax import lax
from jax.sharding import PartitionSpec as P

D = 2048
HEADS = 32
HEAD_DIM = 64
SL = 256
MICRO = 2


EPSILON = 1e-05
ROPE_THETA = 130000.0
MASKED_SCORE = -1000000000.0


def rope_tables(slot_count, head_width):
    half_width = head_width // 2
    frequency = jnp.exp(
        jnp.arange(half_width, dtype=jnp.float32) * (-2.0 * math.log(ROPE_THETA) / head_width)
    )
    angles = jnp.arange(slot_count, dtype=jnp.float32)[:, None] * frequency[None, :]
    return (jnp.cos(angles)[:, None, :], jnp.sin(angles)[:, None, :])


def rotate(values, cosine_table, sine_table):
    half_width = values.shape[-1] // 2
    first_half = values[..., :half_width]
    second_half = values[..., half_width:]
    return jnp.concatenate(
        [
            first_half * cosine_table - second_half * sine_table,
            second_half * cosine_table + first_half * sine_table,
        ],
        axis=-1,
    )


def unrotate(grads, cosine_table, sine_table):
    half_width = grads.shape[-1] // 2
    first_half = grads[..., :half_width]
    second_half = grads[..., half_width:]
    return jnp.concatenate(
        [
            first_half * cosine_table + second_half * sine_table,
            second_half * cosine_table - first_half * sine_table,
        ],
        axis=-1,
    )


def masked_scores(queries, key_rows, length):
    positions = jnp.arange(SL, dtype=jnp.int32)
    allowed = (positions[None, :] <= positions[:, None]) & (positions[None, :] < length)
    scores = jnp.einsum(
        "qhd,khd->hqk", queries, key_rows, preferred_element_type=jnp.float32
    ) * HEAD_DIM ** (-0.5)
    return jnp.where(allowed[None], scores, MASKED_SCORE)


def attend_forward(queries, key_rows, values, length):
    scores = masked_scores(queries, key_rows, length)
    row_top = jnp.max(scores, axis=-1, keepdims=True)
    exp_scores = jnp.exp(scores - row_top)
    row_total = jnp.sum(exp_scores, axis=-1, keepdims=True)
    softmax_out = (exp_scores / row_total).astype(jnp.bfloat16)
    mixed_heads = jnp.einsum(
        "hqk,khd->qhd", softmax_out, values, preferred_element_type=jnp.float32
    )
    return (mixed_heads, row_top + jnp.log(row_total))


def attend_backward(queries, key_rows, values, length, log_total, mixed_grad):
    softmax_out = jnp.exp(masked_scores(queries, key_rows, length) - log_total)
    softmax_grad = jnp.einsum(
        "qhd,khd->hqk", mixed_grad, values, preferred_element_type=jnp.float32
    )
    values_grad = jnp.einsum(
        "hqk,qhd->khd",
        softmax_out.astype(jnp.bfloat16),
        mixed_grad,
        preferred_element_type=jnp.float32,
    )
    row_inner = jnp.sum(softmax_out * softmax_grad, axis=-1, keepdims=True)
    scores_grad = (softmax_out * (softmax_grad - row_inner)).astype(jnp.bfloat16)
    queries_grad = jnp.einsum(
        "hqk,khd->qhd", scores_grad, key_rows, preferred_element_type=jnp.float32
    ) * HEAD_DIM ** (-0.5)
    keys_grad = jnp.einsum(
        "hqk,qhd->khd", scores_grad, queries, preferred_element_type=jnp.float32
    ) * HEAD_DIM ** (-0.5)
    return (queries_grad, keys_grad, values_grad)


def column_gather(values):
    return lax.all_gather(values, "col", axis=1, tiled=True)


def row_scatter(stacked):
    return lax.psum_scatter(stacked, "row", scatter_dimension=2, tiled=True)


def row_gather(stacked):
    return lax.all_gather(stacked, "row", axis=2, tiled=True)


def column_scatter(partial_rows):
    return lax.psum_scatter(
        partial_rows.astype(jnp.bfloat16), "col", scatter_dimension=1, tiled=True
    ).astype(jnp.float32)


def feature_total(row_values):
    return lax.psum(row_values, ("row", "col"))


def norm_scale(values):
    return lax.rsqrt(feature_total(jnp.sum(values * values, axis=1)) / D + EPSILON)


def norm_backward(normed_grad, values, inverse_rms, gain_vector, upstream):
    gain_piece = jnp.sum(normed_grad * values * inverse_rms[:, None], axis=0)
    feature_dot = feature_total(jnp.sum(normed_grad * gain_vector * values, axis=1))
    result = (
        upstream
        + normed_grad * gain_vector * inverse_rms[:, None]
        - values * (inverse_rms**3 * feature_dot / D)[:, None]
    )
    return (result, gain_piece)


def per_device(
    tokens,
    lengths,
    deal_order,
    attention_gain,
    query_weight,
    key_weight,
    value_weight,
    output_weight,
    feed_gain,
    gate_weight,
    up_weight,
    down_weight,
    cotangent,
):
    head_shape = (SL, HEADS // (lax.axis_size("row") * lax.axis_size("col")), HEAD_DIM)
    dealt_rows = lax.all_to_all(
        jnp.take_along_axis(tokens, deal_order[:, :, None, None], axis=1),
        "dp",
        split_axis=1,
        concat_axis=2,
        tiled=True,
    )
    own_order = lax.dynamic_slice_in_dim(deal_order, lax.axis_index("dp"), 1, 1)
    own_lengths = jnp.take_along_axis(lengths, own_order, axis=1)[:, 0]
    cosine_table, sine_table = rope_tables(SL, HEAD_DIM)
    qkv_weights = jnp.stack((query_weight, key_weight, value_weight))
    pair_weights = jnp.stack((gate_weight, up_weight))
    qkv_grad_sum = jnp.zeros(qkv_weights.shape, jnp.float32)
    output_grad_sum = jnp.zeros(output_weight.shape, jnp.float32)
    pair_grad_sum = jnp.zeros(pair_weights.shape, jnp.float32)
    down_grad_sum = jnp.zeros(down_weight.shape, jnp.float32)
    attention_gain_sum = jnp.zeros(attention_gain.shape, jnp.float32)
    feed_gain_sum = jnp.zeros(feed_gain.shape, jnp.float32)
    row_positions = jnp.arange(SL, dtype=jnp.int32)
    output_blocks = []
    grad_blocks = []
    for micro_index in range(MICRO):
        length = own_lengths[micro_index]
        residual_in = dealt_rows[micro_index, 0].astype(jnp.float32)
        upstream = (
            cotangent[micro_index, 0].astype(jnp.float32)
            * (row_positions < length).astype(jnp.float32)[:, None]
        )
        inverse_first = norm_scale(residual_in)
        normed_first = (residual_in * inverse_first[:, None] * attention_gain).astype(jnp.bfloat16)
        normed_first_all = column_gather(normed_first)
        projected = row_scatter(
            jnp.einsum(
                "rd,kde->kre", normed_first_all, qkv_weights, preferred_element_type=jnp.float32
            )
        )
        queries = rotate(projected[0].reshape(head_shape), cosine_table, sine_table).astype(
            jnp.bfloat16
        )
        key_rows = rotate(projected[1].reshape(head_shape), cosine_table, sine_table).astype(
            jnp.bfloat16
        )
        values = projected[2].reshape(head_shape).astype(jnp.bfloat16)
        mixed_heads, log_total = attend_forward(queries, key_rows, values, length)
        mixed_all = row_gather(mixed_heads.reshape(1, SL, -1).astype(jnp.bfloat16))[0]
        middle = residual_in + column_scatter(
            jnp.dot(mixed_all, output_weight, preferred_element_type=jnp.float32)
        )
        inverse_second = norm_scale(middle)
        normed_second = (middle * inverse_second[:, None] * feed_gain).astype(jnp.bfloat16)
        normed_second_all = column_gather(normed_second)
        gate_up = row_scatter(
            jnp.einsum(
                "rd,kde->kre", normed_second_all, pair_weights, preferred_element_type=jnp.float32
            )
        )
        swish_gate = gate_up[0] / (1.0 + jnp.exp(-gate_up[0]))
        hidden = (swish_gate * gate_up[1]).astype(jnp.bfloat16)
        hidden_all = row_gather(hidden[None])[0]
        layer_rows = middle + column_scatter(
            jnp.dot(hidden_all, down_weight, preferred_element_type=jnp.float32)
        )
        output_blocks.append(layer_rows.astype(jnp.bfloat16))
        top_all = column_gather(upstream.astype(jnp.bfloat16))
        down_grad_sum = down_grad_sum + jnp.einsum(
            "rf,rd->fd", hidden_all, top_all, preferred_element_type=jnp.float32
        )
        hidden_grad = row_scatter(
            jnp.einsum("rd,fd->rf", top_all, down_weight, preferred_element_type=jnp.float32)[None]
        )[0]
        sigmoid_gate = 1.0 / (1.0 + jnp.exp(-gate_up[0]))
        gate_grad = (
            hidden_grad * gate_up[1] * sigmoid_gate * (1.0 + gate_up[0] * (1.0 - sigmoid_gate))
        )
        pair_grad_all = row_gather(
            jnp.stack((gate_grad, hidden_grad * swish_gate)).astype(jnp.bfloat16)
        )
        pair_grad_sum = pair_grad_sum + jnp.einsum(
            "rd,kre->kde", normed_second_all, pair_grad_all, preferred_element_type=jnp.float32
        )
        second_grad = column_scatter(
            jnp.einsum(
                "kre,kde->rd", pair_grad_all, pair_weights, preferred_element_type=jnp.float32
            )
        )
        middle_grad, gain_piece = norm_backward(
            second_grad, middle, inverse_second, feed_gain, upstream
        )
        feed_gain_sum = feed_gain_sum + gain_piece
        branch_all = column_gather(middle_grad.astype(jnp.bfloat16))
        output_grad_sum = output_grad_sum + jnp.einsum(
            "rh,rd->hd", mixed_all, branch_all, preferred_element_type=jnp.float32
        )
        mixed_grad = row_scatter(
            jnp.einsum("rd,hd->rh", branch_all, output_weight, preferred_element_type=jnp.float32)[
                None
            ]
        )[0]
        queries_grad, keys_grad, values_grad = attend_backward(
            queries,
            key_rows,
            values,
            length,
            log_total,
            mixed_grad.reshape(head_shape).astype(jnp.bfloat16),
        )
        turned_back = jnp.stack(
            (
                unrotate(queries_grad, cosine_table, sine_table),
                unrotate(keys_grad, cosine_table, sine_table),
                values_grad,
            )
        )
        three_all = row_gather(turned_back.reshape(3, SL, -1).astype(jnp.bfloat16))
        qkv_grad_sum = qkv_grad_sum + jnp.einsum(
            "rd,kre->kde", normed_first_all, three_all, preferred_element_type=jnp.float32
        )
        first_grad = column_scatter(
            jnp.einsum("kre,kde->rd", three_all, qkv_weights, preferred_element_type=jnp.float32)
        )
        input_grad, gain_piece = norm_backward(
            first_grad, residual_in, inverse_first, attention_gain, middle_grad
        )
        attention_gain_sum = attention_gain_sum + gain_piece
        grad_blocks.append(input_grad.astype(jnp.bfloat16))
    reduced = (
        lax.psum_scatter(
            attention_gain_sum.astype(jnp.bfloat16), "dp", scatter_dimension=0, tiled=True
        ).astype(jnp.float32),
        lax.psum_scatter(
            qkv_grad_sum[0].astype(jnp.bfloat16), "dp", scatter_dimension=0, tiled=True
        ).astype(jnp.float32),
        lax.psum_scatter(
            qkv_grad_sum[1].astype(jnp.bfloat16), "dp", scatter_dimension=0, tiled=True
        ).astype(jnp.float32),
        lax.psum_scatter(
            qkv_grad_sum[2].astype(jnp.bfloat16), "dp", scatter_dimension=0, tiled=True
        ).astype(jnp.float32),
        lax.psum_scatter(
            output_grad_sum.astype(jnp.bfloat16), "dp", scatter_dimension=0, tiled=True
        ).astype(jnp.float32),
        lax.psum_scatter(
            feed_gain_sum.astype(jnp.bfloat16), "dp", scatter_dimension=0, tiled=True
        ).astype(jnp.float32),
        lax.psum_scatter(
            pair_grad_sum[0].astype(jnp.bfloat16), "dp", scatter_dimension=0, tiled=True
        ).astype(jnp.float32),
        lax.psum_scatter(
            pair_grad_sum[1].astype(jnp.bfloat16), "dp", scatter_dimension=0, tiled=True
        ).astype(jnp.float32),
        lax.psum_scatter(
            down_grad_sum.astype(jnp.bfloat16), "dp", scatter_dimension=0, tiled=True
        ).astype(jnp.float32),
    )
    returned_out, returned_grad = (
        lax.all_to_all(
            jnp.stack(output_blocks)[:, None], "dp", split_axis=2, concat_axis=1, tiled=True
        ),
        lax.all_to_all(
            jnp.stack(grad_blocks)[:, None], "dp", split_axis=2, concat_axis=1, tiled=True
        ),
    )
    slot_of = jnp.argsort(deal_order, axis=1)[:, :, None, None]
    layer_output = jnp.take_along_axis(returned_out, slot_of, axis=1)
    tokens_grad = jnp.take_along_axis(returned_grad, slot_of, axis=1)
    return (
        layer_output,
        tokens_grad,
        reduced[0],
        reduced[1],
        reduced[2],
        reduced[3],
        reduced[4],
        reduced[5],
        reduced[6],
        reduced[7],
        reduced[8],
    )


def solution(mesh):
    in_specs = (
        P(None, None, "dp", ("row", "col")),
        P(),
        P(),
        P(("row", "col")),
        P("row", "col"),
        P("row", "col"),
        P("row", "col"),
        P("col", "row"),
        P(("row", "col")),
        P("row", "col"),
        P("row", "col"),
        P("col", "row"),
        P(None, "dp", None, ("row", "col")),
    )
    out_specs = (
        P(None, None, "dp", ("row", "col")),
        P(None, None, "dp", ("row", "col")),
        P(("row", "col", "dp")),
        P(("row", "dp"), "col"),
        P(("row", "dp"), "col"),
        P(("row", "dp"), "col"),
        P(("col", "dp"), "row"),
        P(("row", "col", "dp")),
        P(("row", "dp"), "col"),
        P(("row", "dp"), "col"),
        P(("col", "dp"), "row"),
    )
    return jax.shard_map(
        per_device, mesh=mesh, in_specs=in_specs, out_specs=out_specs, check_vma=False
    )
```

profile of v0, /device:TPU:0, one launch (start us, length us, event | category | flops | bytes accessed | tf_op | source)
XLA Modules:
  0.0 1240.4 jit_solution(1370745527233818062)
XLA Ops:
  102.4 10.7 all_gather.60
  121.8 12.0 copy.158
  133.8 12.3 copy.159
  167.8 10.3 convolution_bitcast_fusion
  186.7 9.7 convolution_bitcast_fusion.3
  205.2 11.7 convolution_bitcast_fusion.1
  224.1 10.2 reduce-scatter.38.cloned.1.call-done
  250.8 10.1 fusion.24
  267.1 10.1 fusion.23
  287.7 11.2 reduce-scatter.60.cloned.1.call-done
  298.9 17.5 %reduce-scatter.52.cloned.1.call-done = bf16[256,512]{1,0:T(8,128)(2,1)} async-done(((bf16[256,1024]{1,0:T(8,128)(2,1)}), bf16[256,512]{1,0:T(8,128)(2,1)}) %reduce-scatter.52.cloned.1.call-update) | async-done | bytes 262160 | tf_op jit(solution)/shard_map/reduce_scatter | solution.py:111
  468.3 11.7 add_convert_fusion.1
  481.0 15.7 %fusion.74 = f32[2,4096,1024]{2,1,0:T(8,128)} fusion(bf16[2,256,4096]{1,2,0:T(8,128)(2,1)} %all-gather.11.cloned.1.call-done, bf16[256,1024]{1,0:T(8,128)(2,1)S(1)} %copy-done.32), kind=kOutput, calls=%fused_computation.147 | convolution fusion | flops 4294967296 | bytes 38273024 | tf_op jit(solution)/shard_map/rd,kre->kde/dot_general | solution.py:228
  496.8 19.1 %fusion = bf16[2,1024,4096]{1,2,0:T(8,128)(2,1)} fusion(f32[2,4096,1024]{2,1,0:T(8,128)} %fusion.74, bf16[2,256,4096]{1,2,0:T(8,128)(2,1)S(1)} %copy-done.23, bf16[256,1024]{1,0:T(8,128)(2,1)S(1)} %copy-done.30), kind=kOutput, calls=%fused_computation.5 | convolution fusion | flops 4311744512 | bytes 55050240 | tf_op jit(solution)/shard_map/rd,kre->kde/dot_general | solution.py:228
  515.9 11.7 slice_bitcast_fusion
  527.7 11.3 copy.220
  539.0 11.6 copy.218
  572.2 21.8 %all-to-all-done.1 = bf16[2,1,256,512]{3,0,1,2:T(2,128)(2,1)S(1)} async-done(((bf16[2,1,256,512]{3,0,1,2:T(2,128)(2,1)}), bf16[2,1,256,512]{3,0,1,2:T(2,128)(2,1)S(1)}, u32[]{:S(2)}, u32[]{:S(2)}) %all-to-all-start.1) | async-done | bytes 524320 | tf_op jit(solution)/shard_map/all_to_all | solution.py:306
  601.1 22.1 %all-reduce.6 = (bf16[512]{0:T(512)(128)(2,1)S(1)}, bf16[512]{0:T(512)(128)(2,1)S(1)}) all-reduce(bf16[512]{0:T(512)(128)(2,1)S(1)} %add_convert_fusion.15, bf16[512]{0:T(512)(128)(2,1)S(1)} %add_convert_fusion.14), channel_id=18, replica_groups=mesh['dp'=8,'row'=2,'col'=2] {'dp'}, use_global_device_ids=true, to_apply=%region_41.43.clone | all-reduce | flops 1024 | bytes 4096
  635.0 68.9 %reduce-scatter.72.cloned.1.call-done = bf16[128,1024]{1,0:T(8,128)(2,1)} async-done(((bf16[1024,1024]{1,0:T(8,128)(2,1)}), bf16[128,1024]{1,0:T(8,128)(2,1)}) %reduce-scatter.72.cloned.1.call-update) | async-done | bytes 262160
  705.9 68.8 %reduce-scatter.70.cloned.1.call-done = bf16[128,1024]{1,0:T(8,128)(2,1)} async-done(((bf16[1024,1024]{1,0:T(8,128)(2,1)}), bf16[128,1024]{1,0:T(8,128)(2,1)}) %reduce-scatter.70.cloned.1.call-update) | async-done | bytes 262160
  776.7 149.5 %reduce-scatter.68.cloned.1.call-done = bf16[512,1024]{1,0:T(8,128)(2,1)} async-done(((bf16[4096,1024]{1,0:T(8,128)(2,1)}), bf16[512,1024]{1,0:T(8,128)(2,1)}) %reduce-scatter.68.cloned.1.call-update) | async-done | bytes 1048592 | tf_op jit(solution)/shard_map/reduce_scatter | solution.py:301
  929.0 149.4 %reduce-scatter.78.cloned.1.call-done = bf16[128,4096]{1,0:T(8,128)(2,1)} async-done(((bf16[1024,4096]{1,0:T(8,128)(2,1)}), bf16[128,4096]{1,0:T(8,128)(2,1)}) %reduce-scatter.78.cloned.1.call-update) | async-done | bytes 1048592
  1081.6 148.4 %reduce-scatter.76.cloned.1.call-done = bf16[128,4096]{1,0:T(8,128)(2,1)} async-done(((bf16[1024,4096]{1,0:T(8,128)(2,1)}), bf16[128,4096]{1,0:T(8,128)(2,1)}) %reduce-scatter.76.cloned.1.call-update) | async-done | bytes 1048592
  (410 shorter events, 388.3 us)
Async XLA Ops:
  18.6 62.7 %reduce-scatter.42.cloned.1.call-start = ((), (), s32[]{:S(2)}) async-start(), calls=%async_computation.31 | async-start | bytes 4718592 | tf_op jit(solution)/shard_map/reduce_scatter | solution.py:103
  73.9 72.2 %reduce-scatter.36.cloned.1.call-start = ((), (), s32[]{:S(2)}) async-start(), calls=%async_computation.27 | async-start | bytes 786432 | tf_op jit(solution)/shard_map/reduce_scatter | solution.py:111
  92.7 53.4 %reduce-scatter.44.cloned.1.call-start = ((), (), s32[]{:S(2)}) async-start(), calls=%async_computation.32 | async-start | bytes 786432 | tf_op jit(solution)/shard_map/reduce_scatter | solution.py:111
  101.1 116.4 %reduce-scatter.58.cloned.1.call-start = ((), (), s32[]{:S(2)}) async-start(), calls=%async_computation.42 | async-start | bytes 6291456 | tf_op jit(solution)/shard_map/reduce_scatter | solution.py:103
  121.8 95.7 %reduce-scatter.46.cloned.1.call-start = ((), (), s32[]{:S(2)}) async-start(), calls=%async_computation.33 | async-start | bytes 12582912 | tf_op jit(solution)/shard_map/reduce_scatter | solution.py:103
  178.1 46.0 %reduce-scatter.50.cloned.1.call-start = ((), (), s32[]{:S(2)}) async-start(), calls=%async_computation.36 | async-start | bytes 6291456 | tf_op jit(solution)/shard_map/reduce_scatter | solution.py:103
  196.5 37.8 %reduce-scatter.38.cloned.1.call-start = ((), (), s32[]{:S(2)}) async-start(), calls=%async_computation.28 | async-start | bytes 12582912 | tf_op jit(solution)/shard_map/reduce_scatter | solution.py:103
  224.0 43.1 %all-gather.11.cloned.1.call-start = ((), (), s32[]{:S(2)}) async-start(), calls=%async_computation.37 | async-start | bytes 6291456 | tf_op jit(solution)/shard_map/all_gather | solution.py:107
  240.8 39.6 %all-gather.9.cloned.1.call-start = ((), (), s32[]{:S(2)}) async-start(), calls=%async_computation.34 | async-start | bytes 3145728 | tf_op jit(solution)/shard_map/all_gather | solution.py:107
  241.5 57.3 %reduce-scatter.60.cloned.1.call-start = ((), (), s32[]{:S(2)}) async-start(), calls=%async_computation.44 | async-start | bytes 786432 | tf_op jit(solution)/shard_map/reduce_scatter | solution.py:111
  261.0 55.4 %reduce-scatter.52.cloned.1.call-start = ((), (), s32[]{:S(2)}) async-start(), calls=%async_computation.38 | async-start | bytes 786432 | tf_op jit(solution)/shard_map/reduce_scatter | solution.py:111
  277.2 56.3 %reduce-scatter.48.cloned.1.call-start = ((), (), s32[]{:S(2)}) async-start(), calls=%async_computation.35 | async-start | bytes 786432 | tf_op jit(solution)/shard_map/reduce_scatter | solution.py:111
  287.6 72.9 %reduce-scatter.54.cloned.1.call-start = ((), (), s32[]{:S(2)}) async-start(), calls=%async_computation.39 | async-start | bytes 1572864 | tf_op jit(solution)/shard_map/reduce_scatter | solution.py:103
  358.1 45.5 %all-gather.13.cloned.1.call-start = ((), (), s32[]{:S(2)}) async-start(), calls=%async_computation.40 | async-start | bytes 2359296 | tf_op jit(solution)/shard_map/all_gather | solution.py:107
  403.6 147.2 %reduce-scatter.56.cloned.1.call-start = ((), (), s32[]{:S(2)}) async-start(), calls=%async_computation.41 | async-start | bytes 786432 | tf_op jit(solution)/shard_map/reduce_scatter | solution.py:111
  408.9 141.8 %reduce-scatter.64.cloned.1.call-start = ((), (), s32[]{:S(2)}) async-start(), calls=%async_computation.47 | async-start | bytes 786432 | tf_op jit(solution)/shard_map/reduce_scatter | solution.py:111
  419.1 141.5 %reduce-scatter.40.cloned.1.call-start = ((), (), s32[]{:S(2)}) async-start(), calls=%async_computation.30 | async-start | bytes 786432 | tf_op jit(solution)/shard_map/reduce_scatter | solution.py:111
  434.4 164.9 %reduce-scatter.66.cloned.1.call-start = ((), (), s32[]{:S(2)}) async-start(), calls=%async_computation.48 | async-start | bytes 2359296 | tf_op jit(solution)/shard_map/reduce_scatter | solution.py:289
  437.7 195.2 %reduce-scatter.74.cloned.1.call-start = ((), (), s32[]{:S(2)}) async-start(), calls=%async_computation.52 | async-start | bytes 2359296
  450.7 253.1 %reduce-scatter.72.cloned.1.call-start = ((), (), s32[]{:S(2)}) async-start(), calls=%async_computation.51 | async-start | bytes 2359296
  454.7 319.9 %reduce-scatter.70.cloned.1.call-start = ((), (), s32[]{:S(2)}) async-start(), calls=%async_computation.50 | async-start | bytes 2359296
  457.4 468.8 %reduce-scatter.68.cloned.1.call-start = ((), (), s32[]{:S(2)}) async-start(), calls=%async_computation.49 | async-start | bytes 9437184 | tf_op jit(solution)/shard_map/reduce_scatter | solution.py:301
  480.0 598.4 %reduce-scatter.78.cloned.1.call-start = ((), (), s32[]{:S(2)}) async-start(), calls=%async_computation.54 | async-start | bytes 9437184
  539.0 691.1 %reduce-scatter.76.cloned.1.call-start = ((), (), s32[]{:S(2)}) async-start(), calls=%async_computation.53 | async-start | bytes 9437184
  (94 other events, 825.1 us)
Sparse Core Ops, SparseCore 0:
  92.8 16.9 reduce-scatter.35
  112.6 14.3 reduce-scatter.43
  129.1 12.0 reduce-scatter.57
  178.2 17.2 reduce-scatter.45
  197.9 13.2 reduce-scatter.49
  217.1 17.1 reduce-scatter.37
  235.8 14.9 all-gather.14
  252.2 14.8 all-gather.10
  268.6 11.7 all-gather.8
  283.1 15.7 reduce-scatter.59
  301.8 14.5 reduce-scatter.51
  319.0 14.5 reduce-scatter.47
  402.9 10.8 all-gather.16
  415.4 11.7 all-gather.6
  429.9 15.7 reduce-scatter.55
  448.5 14.5 reduce-scatter.63
  466.0 14.5 reduce-scatter.39
  484.1 67.7 reduce-scatter.65
  555.3 77.5 reduce-scatter.73
  637.0 66.7 reduce-scatter.71
  707.8 66.8 reduce-scatter.69
  778.2 148.0 reduce-scatter.67
  930.3 148.0 reduce-scatter.77
  1082.0 147.9 reduce-scatter.75
  (5 shorter events, 46.1 us)
where the time goes:
time: 1250 us; the launch traced here: 1240 us
  waiting for transfers between devices  693 us (55%)
  matrix products  182 us (15%)
  local copies, waits for them, and re-layouts  140 us (11%)
  blocking collectives  125 us (10%)
  other arithmetic  65.1 us (5%)
  starting transfers between devices  19.2 us (2%)
  between operations  16.4 us (1%)
    unnamed x34, waiting for transfers between devices  443 us
    reduce_scatter x1, waiting for transfers between devices, per_device(): lax.psum_scatter(down_grad_sum.astype(jnp.bfloat16), 'dp', scatter_dimens...  149 us
    unnamed x195, local copies, waits for them, and re-layouts  97.5 us
    all_gather x8, blocking collectives, column_gather(): return lax.all_gather(values, 'col', axis=1, tiled=True)  69 us
    dot_general x2, matrix products, per_device(): jnp.einsum('rd,kre->kde', normed_second_all, pair_grad_all, preferred_ele...  34.9 us
    reduce_scatter x8, waiting for transfers between devices, column_scatter(): lax.psum_scatter(partial_rows.astype(jnp.bfloat16), 'col', scatter_dimens...  34.2 us
    all_gather x6, waiting for transfers between devices, row_gather(): return lax.all_gather(stacked, 'row', axis=2, tiled=True)  31.3 us
    psum x4, blocking collectives, feature_total(): return lax.psum(row_values, ('row', 'col'))  29.1 us
  transfers between devices with their start and end apart: 32, of which 17 were waited for; matrix products, arithmetic and copies ran while one was open for 26% of the time, Pallas kernels for 0%

commit v1 on v0

v1 whole, which is shorter than its diff:
```python
import math

import jax
import jax.numpy as jnp
from jax import lax
from jax.experimental import pallas as pl
from jax.experimental.pallas import tpu as pltpu
from jax.sharding import PartitionSpec as P

D = 2048
HEADS = 32
HEAD_DIM = 64
SL = 256
MICRO = 2
ROWS = MICRO * SL

EPSILON = 1e-05
ROPE_THETA = 130000.0
MASKED_SCORE = -1000000000.0
F32 = jnp.float32
BF16 = jnp.bfloat16
SWAP = [(0, 1), (1, 0)]


def mm(a, b):
    return jnp.dot(a, b, preferred_element_type=F32)


def mm_nt(a, b):
    return lax.dot_general(a, b, (((1,), (1,)), ((), ())), preferred_element_type=F32)


def mm_tn(a, b):
    return lax.dot_general(a, b, (((0,), (0,)), ((), ())), preferred_element_type=F32)


def rope_tables():
    half = HEAD_DIM // 2
    frequency = jnp.exp(
        jnp.arange(half, dtype=F32) * (-2.0 * math.log(ROPE_THETA) / HEAD_DIM)
    )
    angles = jnp.arange(SL, dtype=F32)[:, None] * frequency[None, :]
    cosine = jnp.cos(angles)
    sine = jnp.sin(angles)
    zero = jnp.zeros_like(sine)
    table_cos = jnp.concatenate([cosine] * 4, axis=1)
    table_first = jnp.concatenate([sine, zero] * 2, axis=1)
    table_second = jnp.concatenate([zero, sine] * 2, axis=1)
    return table_cos, table_first, table_second


def turn(v, cos, first, second):
    ahead = pltpu.roll(v, 128 - HEAD_DIM // 2, 1)
    behind = pltpu.roll(v, HEAD_DIM // 2, 1)
    return v * cos - ahead * first + behind * second


def turn_back(v, cos, first, second):
    ahead = pltpu.roll(v, 128 - HEAD_DIM // 2, 1)
    behind = pltpu.roll(v, HEAD_DIM // 2, 1)
    return v * cos + ahead * first - behind * second


def head_mask(head):
    lane = lax.broadcasted_iota(jnp.int32, (SL, 128), 1)
    return (lane // HEAD_DIM) == head


def softmax_of(q, k, allowed):
    scores = mm_nt(q, k) * HEAD_DIM ** (-0.5)
    scores = jnp.where(allowed, scores, MASKED_SCORE)
    exps = jnp.exp(scores - jnp.max(scores, axis=1, keepdims=True))
    return exps / jnp.sum(exps, axis=1, keepdims=True)


def allowed_of(length):
    query = lax.broadcasted_iota(jnp.int32, (SL, SL), 0)
    key = lax.broadcasted_iota(jnp.int32, (SL, SL), 1)
    return (key <= query) & (key < length)


def attend_kernel(len_ref, q_ref, k_ref, v_ref, cos_ref, first_ref, second_ref, o_ref, qr_ref, kr_ref, vr_ref):
    cos, first, second = cos_ref[...], first_ref[...], second_ref[...]
    qr = turn(q_ref[...], cos, first, second).astype(BF16)
    kr = turn(k_ref[...], cos, first, second).astype(BF16)
    vr = v_ref[...].astype(BF16)
    qr_ref[...] = qr
    kr_ref[...] = kr
    vr_ref[...] = vr
    allowed = allowed_of(len_ref[pl.program_id(0)])
    out = jnp.zeros((SL, 128), F32)
    for head in range(2):
        mask = head_mask(head)
        probs = softmax_of(jnp.where(mask, qr, jnp.zeros_like(qr)), kr, allowed).astype(BF16)
        out = out + mm(probs, jnp.where(mask, vr, jnp.zeros_like(vr)))
    o_ref[...] = out.astype(BF16)


def attend_grad_kernel(
    len_ref, qr_ref, kr_ref, vr_ref, od_ref, cos_ref, first_ref, second_ref, dq_ref, dk_ref, dv_ref
):
    cos, first, second = cos_ref[...], first_ref[...], second_ref[...]
    qr, kr, vr, od = qr_ref[...], kr_ref[...], vr_ref[...], od_ref[...]
    allowed = allowed_of(len_ref[pl.program_id(0)])
    dq = jnp.zeros((SL, 128), F32)
    dk = jnp.zeros((SL, 128), F32)
    dv = jnp.zeros((SL, 128), F32)
    zero = jnp.zeros_like(qr)
    for head in range(2):
        mask = head_mask(head)
        q_own = jnp.where(mask, qr, zero)
        k_own = jnp.where(mask, kr, zero)
        od_own = jnp.where(mask, od, zero)
        probs = softmax_of(q_own, kr, allowed)
        d_probs = mm_nt(od_own, vr)
        dv = dv + mm_tn(probs.astype(BF16), od_own)
        inner = jnp.sum(probs * d_probs, axis=1, keepdims=True)
        d_scores = (probs * (d_probs - inner)).astype(BF16)
        dq = dq + mm(d_scores, k_own)
        dk = dk + mm_tn(d_scores, q_own)
    scale = HEAD_DIM ** (-0.5)
    dq_ref[...] = turn_back(dq * scale, cos, first, second).astype(BF16)
    dk_ref[...] = turn_back(dk * scale, cos, first, second).astype(BF16)
    dv_ref[...] = dv.astype(BF16)


def attention_specs(width):
    pairs = width // 128

    def part(index):
        return pl.BlockSpec((SL, 128), lambda m, h, lens: (m, index * pairs + h))

    table = pl.BlockSpec((SL, 128), lambda m, h, lens: (0, 0))
    return pairs, part, table


def attend_forward(lengths, qkv, tables):
    width = qkv.shape[1] // 3
    pairs, part, table = attention_specs(width)
    shape = jax.ShapeDtypeStruct((ROWS, width), BF16)
    return pl.pallas_call(
        attend_kernel,
        out_shape=(shape,) * 4,
        grid_spec=pltpu.PrefetchScalarGridSpec(
            num_scalar_prefetch=1,
            grid=(MICRO, pairs),
            in_specs=[part(0), part(1), part(2), table, table, table],
            out_specs=[part(0)] * 4,
        ),
        cost_estimate=pl.CostEstimate(
            flops=ROWS * SL * width * 4, bytes_accessed=ROWS * width * 20, transcendentals=0
        ),
    )(lengths, qkv, qkv, qkv, *tables)


def attend_backward(lengths, qr, kr, vr, od, tables):
    width = qr.shape[1]
    pairs, part, table = attention_specs(width)
    shape = jax.ShapeDtypeStruct((ROWS, width), BF16)
    return pl.pallas_call(
        attend_grad_kernel,
        out_shape=(shape,) * 3,
        grid_spec=pltpu.PrefetchScalarGridSpec(
            num_scalar_prefetch=1,
            grid=(MICRO, pairs),
            in_specs=[part(0)] * 4 + [table] * 3,
            out_specs=[part(0)] * 3,
        ),
        cost_estimate=pl.CostEstimate(
            flops=ROWS * SL * width * 10, bytes_accessed=ROWS * width * 14, transcendentals=0
        ),
    )(lengths, qr, kr, vr, od, *tables)


def per_device(
    tokens,
    lengths,
    deal_order,
    attention_gain,
    query_weight,
    key_weight,
    value_weight,
    output_weight,
    feed_gain,
    gate_weight,
    up_weight,
    down_weight,
    cotangent,
):
    groups = lax.axis_size("dp")
    line = groups // 2
    dp = lax.axis_index("dp")
    row = lax.axis_index("row")
    col = lax.axis_index("col")
    z, x = dp // 2, dp % 2
    half = D // 2
    block = D // 4

    def over_row(v):
        return lax.ppermute(v, "row", SWAP)

    def over_col(v):
        return lax.ppermute(v, "col", SWAP)

    def over_x(v):
        return lax.ppermute(v, "dp", [(i, i ^ 1) for i in range(groups)])

    def ordered(own, other, index, axis=-1):
        return jnp.where(
            index == 0,
            jnp.concatenate([own, other], axis=axis),
            jnp.concatenate([other, own], axis=axis),
        )

    def halves(v, axis):
        size = v.shape[axis] // 2
        own = lax.dynamic_slice_in_dim(v, row * size, size, axis)
        other = lax.dynamic_slice_in_dim(v, (1 - row) * size, size, axis)
        return own, other

    def x_parts(v, width):
        even = jnp.concatenate(
            [v[:, s : s + width] for s in range(0, v.shape[1], 2 * width)], axis=1
        )
        odd = jnp.concatenate(
            [v[:, s : s + width] for s in range(width, v.shape[1], 2 * width)], axis=1
        )
        return jnp.where(x == 0, even, odd), jnp.where(x == 0, odd, even)

    def line_sum(grads, index_of):
        size = grads.shape[0] // line

        def chunk(dest):
            at = index_of(jnp.clip(dest, 0, line - 1))
            return lax.dynamic_slice_in_dim(grads, at * size, size, 0)

        right = left = None
        for step in range(line - 1):
            send_right = chunk(line - 1 - step + z)
            send_left = chunk(step - (line - 1 - z))
            if step:
                send_right = (send_right.astype(F32) + right.astype(F32)).astype(BF16)
                send_left = (send_left.astype(F32) + left.astype(F32)).astype(BF16)
            rights = [
                (2 * i + k, 2 * i + 2 + k) for i in range(min(step, line - 2) + 1) for k in range(2)
            ]
            lefts = [(2 * (line - 1) + 1 - a, 2 * (line - 1) + 1 - b) for a, b in rights]
            right = lax.ppermute(send_right, "dp", rights)
            left = lax.ppermute(send_left, "dp", lefts)
        return chunk(z).astype(F32) + right.astype(F32) + left.astype(F32)

    def plain_index(dest):
        return dest

    def row_index(dest):
        return lax.rem(dest + line - row * (line // 2), line)

    dealt = lax.all_to_all(
        jnp.take_along_axis(tokens, deal_order[:, :, None, None], axis=1),
        "dp",
        split_axis=1,
        concat_axis=2,
        tiled=True,
    )
    own_order = lax.dynamic_slice_in_dim(deal_order, dp, 1, 1)
    own_lengths = jnp.take_along_axis(lengths, own_order, axis=1)[:, 0]
    tables = rope_tables()
    live = (jnp.arange(SL, dtype=jnp.int32)[None, :] < own_lengths[:, None]).reshape(ROWS, 1)
    top_block = jnp.where(live, cotangent.reshape(ROWS, block), 0.0).astype(BF16)

    gains = jnp.stack([attention_gain, feed_gain])
    gains_half = ordered(gains, over_col(gains), col)
    gains_other = over_row(gains_half)
    gains_full = jnp.concatenate([gains_half, gains_other], axis=1)

    x_block = dealt.reshape(ROWS, block)
    x_half = ordered(x_block, over_col(x_block), col)
    x_other = over_row(x_half)

    own, other = [], []
    for w in (query_weight, key_weight, value_weight):
        a, b = halves(w, 1)
        own.append(a)
        other.append(b)
    qkv_w = jnp.concatenate(
        [jnp.concatenate(own, axis=1), over_row(jnp.concatenate(other, axis=1))], axis=0
    )
    a, b = halves(output_weight, 0)
    out_w = jnp.concatenate([a, over_row(b)], axis=1)
    gate_own, gate_other = halves(gate_weight, 1)
    up_own, up_other = halves(up_weight, 1)
    pair_w = jnp.concatenate(
        [
            jnp.concatenate([gate_own, up_own], axis=1),
            over_row(jnp.concatenate([gate_other, up_other], axis=1)),
        ],
        axis=0,
    )
    a, b = halves(down_weight, 0)
    down_w = jnp.concatenate([a, over_row(b)], axis=1)

    top_half = ordered(top_block, over_col(top_block), col)
    top_full = jnp.concatenate([top_half, over_row(top_half)], axis=1)
    top_pair = jnp.concatenate([top_half, over_x(top_half)], axis=0)
    hidden_grad = mm_nt(top_full, down_w)

    x_full = jnp.concatenate([x_half, x_other], axis=1).astype(F32)
    inverse_first = lax.rsqrt(jnp.mean(x_full * x_full, axis=1, keepdims=True) + EPSILON)
    normed_first = (x_full * inverse_first * gains_full[0][None, :]).astype(BF16)
    qkv = mm(normed_first, qkv_w)
    mixed, qr, kr, vr = attend_forward(own_lengths, qkv, tables)
    partial = mm(mixed, out_w)
    summed = (partial[:, :half] + over_row(partial[:, half:].astype(BF16)).astype(F32)).astype(BF16)
    middle = x_half.astype(F32) + (summed.astype(F32) + over_col(summed).astype(F32))

    middle_low = middle.astype(BF16)
    middle_full = jnp.concatenate([middle_low, over_row(middle_low)], axis=1).astype(F32)
    inverse_second = lax.rsqrt(
        jnp.mean(middle_full * middle_full, axis=1, keepdims=True) + EPSILON
    )
    normed_second = (middle_full * inverse_second * gains_full[1][None, :]).astype(BF16)
    gate_up = mm(normed_second, pair_w)
    quarter = gate_up.shape[1] // 2
    gate, up = gate_up[:, :quarter], gate_up[:, quarter:]
    sigmoid = 1.0 / (1.0 + jnp.exp(-gate))
    swish = gate * sigmoid
    hidden = (swish * up).astype(BF16)
    gate_grad = (hidden_grad * up * sigmoid * (1.0 + gate * (1.0 - sigmoid))).astype(BF16)
    up_grad = (hidden_grad * swish).astype(BF16)

    def side_grad(values, others):
        width = 2 * values.shape[1] // groups
        mine, theirs = x_parts(values, width)
        pair = jnp.concatenate([mine, over_x(theirs)], axis=0)
        both = jnp.concatenate([pair, over_row(pair)], axis=1)
        return line_sum(mm_tn(both, others).astype(BF16), row_index)

    down_sum = side_grad(hidden, top_pair)

    def width_pair(values):
        mine, theirs = x_parts(values, values.shape[1] // groups)
        return jnp.concatenate([mine, over_x(theirs)], axis=0)

    def inner_grad(left_pair, values):
        pair = jnp.concatenate([values, over_x(values)], axis=0)
        both = jnp.concatenate([pair, over_row(pair)], axis=1)
        return line_sum(mm_tn(left_pair, both).astype(BF16), plain_index)

    def columns_in_order(v):
        size = v.shape[1] // 2
        return ordered(v[:, :size], v[:, size:], row)

    second_pair = width_pair(normed_second[:, :half])
    gate_sum = columns_in_order(inner_grad(second_pair, gate_grad))
    up_sum = columns_in_order(inner_grad(second_pair, up_grad))

    partial = mm_nt(jnp.concatenate([gate_grad, up_grad], axis=1), pair_w)
    summed = (partial[:, :half] + over_row(partial[:, half:].astype(BF16)).astype(F32)).astype(BF16)
    second_grad = summed.astype(F32) + over_col(summed).astype(F32)
    feed_piece = jnp.sum(second_grad * middle * inverse_second, axis=0)
    scaled = second_grad * gains_half[1][None, :]
    dot = jnp.sum(scaled * middle, axis=1, keepdims=True)
    dot = dot + over_row(dot)
    middle_grad = (
        top_half.astype(F32) + scaled * inverse_second - middle * (inverse_second**3 * dot / D)
    )
    branch = middle_grad.astype(BF16)
    branch_full = jnp.concatenate([branch, over_row(branch)], axis=1)
    mixed_grad = mm_nt(branch_full, out_w).astype(BF16)
    dq, dk, dv = attend_backward(own_lengths, qr, kr, vr, mixed_grad, tables)
    dqkv = jnp.concatenate([dq, dk, dv], axis=1)

    branch_pair = jnp.concatenate([branch, over_x(branch)], axis=0)
    output_sum = side_grad(mixed, branch_pair)

    def own_block(v):
        return lax.dynamic_slice_in_dim(v, col * block, block, 1)

    def block_sum(partial):
        summed = partial[:, :half] + over_row(partial[:, half:].astype(BF16)).astype(F32)
        theirs = lax.dynamic_slice_in_dim(summed, (1 - col) * block, block, 1)
        return own_block(summed) + over_col(theirs.astype(BF16)).astype(F32)

    first_grad = block_sum(mm_nt(dqkv, qkv_w))
    x_own = x_block.astype(F32)
    gain_own = own_block(gains_half)
    attention_piece = jnp.sum(first_grad * x_own * inverse_first, axis=0)
    scaled = first_grad * gain_own[0][None, :]
    dot = jnp.sum(scaled * x_own, axis=1, keepdims=True)
    dot = dot + over_row(dot)
    dot = dot + over_col(dot)
    input_grad = (
        own_block(middle_grad) + scaled * inverse_first - x_own * (inverse_first**3 * dot / D)
    )

    first_pair = width_pair(normed_first[:, :half])
    pieces = inner_grad(first_pair, dqkv)
    size = dq.shape[1]
    mine, theirs = pieces[:, : 3 * size], pieces[:, 3 * size :]
    qkv_sums = [
        ordered(mine[:, k * size : (k + 1) * size], theirs[:, k * size : (k + 1) * size], row)
        for k in range(3)
    ]

    layer_block = own_block(middle) + block_sum(mm(hidden, down_w))

    gain_sums = lax.psum(
        jnp.stack([attention_piece, own_block(feed_piece[None])[0]]), "dp"
    )
    gain_size = block // groups
    gain_sums = lax.dynamic_slice_in_dim(gain_sums, dp * gain_size, gain_size, 1)

    slot_of = jnp.argsort(deal_order, axis=1)[:, :, None, None]

    def returned(v):
        back = lax.all_to_all(
            v.astype(BF16).reshape(MICRO, 1, SL, block), "dp", split_axis=2, concat_axis=1, tiled=True
        )
        return jnp.take_along_axis(back, slot_of, axis=1)

    return (
        returned(layer_block),
        returned(input_grad),
        gain_sums[0],
        qkv_sums[0],
        qkv_sums[1],
        qkv_sums[2],
        output_sum,
        gain_sums[1],
        gate_sum,
        up_sum,
        down_sum,
    )


def solution(mesh):
    in_specs = (
        P(None, None, "dp", ("row", "col")),
        P(),
        P(),
        P(("row", "col")),
        P("row", "col"),
        P("row", "col"),
        P("row", "col"),
        P("col", "row"),
        P(("row", "col")),
        P("row", "col"),
        P("row", "col"),
        P("col", "row"),
        P(None, "dp", None, ("row", "col")),
    )
    out_specs = (
        P(None, None, "dp", ("row", "col")),
        P(None, None, "dp", ("row", "col")),
        P(("row", "col", "dp")),
        P(("row", "dp"), "col"),
        P(("row", "dp"), "col"),
        P(("row", "dp"), "col"),
        P(("col", "dp"), "row"),
        P(("row", "col", "dp")),
        P(("row", "dp"), "col"),
        P(("row", "dp"), "col"),
        P(("col", "dp"), "row"),
    )
    return jax.shard_map(
        per_device, mesh=mesh, in_specs=in_specs, out_specs=out_specs, check_vma=False
    )
```

time: 1250 us -> 759 us (0.61)
  the two profiles are of different devices: /device:TPU:0 before, /device:TPU:8 now
where the time goes in v1:
time: 759 us; the launch traced here: 753 us
  waiting for transfers between devices  324 us (43%)
  matrix products  152 us (20%)
  starting transfers between devices  97 us (13%)
  other arithmetic  82.3 us (11%)
  local copies, waits for them, and re-layouts  52.1 us (7%)
  blocking collectives  23 us (3%)
  Pallas kernels  20.6 us (3%)
    ppermute x15, waiting for transfers between devices, line_sum(): right = lax.ppermute(send_right, 'dp', rights)  157 us
    dot_general x4, matrix products, mm_nt(): lax.dot_general(a, b, (((1,), (1,)), ((), ())), preferred_element_type=F32)  75.2 us
    ppermute x15, waiting for transfers between devices, line_sum(): left = lax.ppermute(send_left, 'dp', lefts)  55 us
    ppermute x9, waiting for transfers between devices, over_x(): return lax.ppermute(v, 'dp', [(i, i ^ 1) for i in range(groups)])  54.5 us
    ppermute x8, waiting for transfers between devices, over_col(): return lax.ppermute(v, 'col', SWAP)  50.6 us
    dot_general x4, matrix products, mm(): return jnp.dot(a, b, preferred_element_type=F32)  44.4 us
    ppermute x15, starting transfers between devices, line_sum(): right = lax.ppermute(send_right, 'dp', rights)  35.9 us
    dot_general x5, matrix products, mm_tn(): lax.dot_general(a, b, (((0,), (0,)), ((), ())), preferred_element_type=F32)  32.2 us
  transfers between devices with their start and end apart: 70, of which 26 were waited for; matrix products, arithmetic and copies ran while one was open for 37% of the time, Pallas kernels for 3%

profile of v1, /device:TPU:8, one launch (start us, length us, event | category | flops | bytes accessed | tf_op | source)
XLA Modules:
  0.0 752.5 jit_solution(12247074571719141911)
XLA Ops:
  24.3 12.7 %constant_dynamic-slice_fusion.16 = (bf16[1024,2048]{1,0:T(8,128)(2,1)}, bf16[1024,2048]{1,0:T(8,128)(2,1)}, bf16[1024,2048]{1,0:T(8,128)(2,1)}, bf16[1024,2048]{1,0:T(8,128)(2,1)}) fusion(bf16[1024,4096]{1,0:T(8,128)(2,1)} %param.25, s32[]{:T(128)S(6)} %select_n.248, s32[]{:T(128)S(6)} %select_n.249, bf16[1024,4096]{1,0:T(8,128)(2,1)} %param.24), kind=kLoop, calls=%fused_computation.199 | loop fusion | bytes 33554440 | tf_op jit(solution)/shard_map/dynamic_slice | solution.py:217
  63.9 20.8 %fusion.75.q_ref.k_ref.v_ref = f32[512,1536]{1,0:T(8,128)} fusion(bf16[512,2048]{1,0:T(8,128)(2,1)S(1)} %fusion.33, bf16[1024,1536]{1,0:T(8,128)(2,1)} %collective-permute-done.4, bf16[1024,512]{1,0:T(8,128)(2,1)S(1)} %copy-done.30, bf16[1024,512]{1,0:T(8,128)(2,1)S(1)} %copy-done.32, bf16[1024,512]{1,0:T(8,128)(2,1)S(1)} %copy-done.28), kind=kOutput, calls=%fused_computation.125 | convolution fusion | flops 3246391296 | bytes 11534336 | tf_op jit(solution)/shard_map/dot_general | solution.py:26
  84.7 9.3 %shard_map.212 = (bf16[512,512]{1,0:T(8,128)(2,1)}, bf16[512,512]{1,0:T(8,128)(2,1)}, bf16[512,512]{1,0:T(8,128)(2,1)}, bf16[512,512]{1,0:T(8,128)(2,1)}) custom-call(s32[2]{0:T(128)} %fusion.96.len_ref, f32[512,1536]{1,0:T(8,128)} %fusion.75.q_ref.k_ref.v_ref, f32[512,1536]{1,0:T(8,128)} %fusion.75.q_ref.k_ref.v_ref, f32[512,1536]{1,0:T(8,128)} %fusion.75.q_ref.k_ref.v_ref, ...), custom_call_target="tpu_custom_call" | custom-call | flops 268435456 | bytes 5242880 | tf_op jit(solution)/shard_map/pallas_call | solution.py:141
  102.4 23.8 %collective-permute-done.7 = bf16[512,1024]{1,0:T(8,128)(2,1)} collective-permute-done((bf16[512,1024]{1,0:T(8,128)(2,1)S(1)}, bf16[512,1024]{1,0:T(8,128)(2,1)}, u32[]{:S(2)}, u32[]{:S(2)}) %collective-permute-start.7) | collective-permute-done | bytes 1048608 | tf_op jit(solution)/shard_map/ppermute | solution.py:203
  149.4 16.1 %fusion.13 = f32[512,4096]{1,0:T(8,128)} fusion(bf16[512,2048]{1,0:T(8,128)(2,1)} %fusion.36, bf16[1024,4096]{1,0:T(8,128)(2,1)} %collective-permute-done.9, bf16[1024,2048]{1,0:T(8,128)(2,1)} %get-tuple-element.43, bf16[1024,2048]{1,0:T(8,128)(2,1)} %get-tuple-element.130), kind=kOutput, calls=%fused_computation.20 | convolution fusion | flops 8640266240 | bytes 27262976 | tf_op jit(solution)/shard_map/dot_general | solution.py:26
  165.5 12.2 %multiply_convert_fusion.1 = (bf16[512,2048]{1,0:T(8,128)(2,1)}, bf16[512,2048]{1,0:T(8,128)(2,1)}, bf16[512,2048]{1,0:T(8,128)(2,1)}) fusion(f32[512,4096]{1,0:T(8,128)} %fusion.13, bf16[2048,1024]{1,0:T(8,128)(2,1)} %collective-permute-done.10, bf16[2048,1024]{1,0:T(8,128)(2,1)} %get-tuple-element.39, bf16[512,1024]{1,0:T(8,128)(2,1)} %collective-permute-done.14, ...), kind=kOutput, calls=%fused_computation.55 | convolution fusion | flops 4331667456 | bytes 25165824 | tf_op jit(solution)/shard_map/dot_general | solution.py:30
  177.7 38.0 %fusion.12 = f32[512,2048]{1,0:T(8,128)S(1)} fusion(bf16[1024,4096]{1,0:T(8,128)(2,1)} %collective-permute-done.9, bf16[1024,2048]{1,0:T(8,128)(2,1)S(1)} %copy-done.11, bf16[1024,2048]{1,0:T(8,128)(2,1)S(1)} %copy-done.12, bf16[512,2048]{1,0:T(8,128)(2,1)} %get-tuple-element.37, bf16[512,2048]{1,0:T(8,128)(2,1)} %get-tuple-element.36), kind=kOutput, calls=%fused_computation.19 | convolution fusion | flops 8648654848 | bytes 25165824 | tf_op jit(solution)/shard_map/dot_general | solution.py:30
  230.1 19.0 %collective-permute-done.16 = bf16[512,1024]{1,0:T(8,128)(2,1)S(1)} collective-permute-done((bf16[512,1024]{1,0:T(8,128)(2,1)S(1)}, bf16[512,1024]{1,0:T(8,128)(2,1)S(1)}, u32[]{:S(2)}, u32[]{:S(2)}) %collective-permute-start.16) | collective-permute-done | bytes 1048608 | tf_op jit(solution)/shard_map/ppermute | solution.py:203
  257.7 40.4 %collective-permute-done.58 = bf16[512,1024]{1,0:T(8,128)(2,1)S(1)} collective-permute-done((bf16[512,1024]{1,0:T(8,128)(2,1)S(1)}, bf16[512,1024]{1,0:T(8,128)(2,1)S(1)}, u32[]{:S(2)}, u32[]{:S(2)}) %collective-permute-start.58) | collective-permute-done | bytes 1048608 | tf_op jit(solution)/shard_map/ppermute | solution.py:206
  313.3 11.6 %collective-permute-done.34 = bf16[512,1024]{1,0:T(8,128)(2,1)} collective-permute-done((bf16[512,1024]{1,0:T(8,128)(2,1)}, bf16[512,1024]{1,0:T(8,128)(2,1)}, u32[]{:S(2)}, u32[]{:S(2)}) %collective-permute-start.34) | collective-permute-done | bytes 1048608 | tf_op jit(solution)/shard_map/ppermute | solution.py:206
  333.3 11.2 %shard_map.213 = (bf16[512,512]{1,0:T(8,128)(2,1)}, bf16[512,512]{1,0:T(8,128)(2,1)}, bf16[512,512]{1,0:T(8,128)(2,1)}) custom-call(s32[2]{0:T(128)} %fusion.96.len_ref, bf16[512,512]{1,0:T(8,128)(2,1)} %get-tuple-element.22.qr_ref, bf16[512,512]{1,0:T(8,128)(2,1)} %get-tuple-element.23.kr_ref, bf16[512,512]{1,0:T(8,128)(2,1)} %get-tuple-element.24.vr_ref, ...), custom_call_target="tpu_custom_call" | custom-call | flops 671088640 | bytes 3670016 | tf_op jit(solution)/shard_map/pallas_call | solution.py:160
  350.4 21.0 %fusion.74 = f32[512,2048]{1,0:T(8,128)S(1)} fusion(bf16[512,1536]{1,0:T(8,128)(2,1)} %constant_dynamic-update-slice_fusion, bf16[1024,1536]{1,0:T(8,128)(2,1)} %collective-permute-done.4, bf16[1024,512]{1,0:T(8,128)(2,1)S(1)} %copy-done.31, bf16[1024,512]{1,0:T(8,128)(2,1)S(1)} %copy-done.33, bf16[1024,512]{1,0:T(8,128)(2,1)S(1)} %copy-done.29), kind=kOutput, calls=%fused_computation.124 | convolution fusion | flops 3246391296 | bytes 12058624 | tf_op jit(solution)/shard_map/dot_general | solution.py:30
  402.1 16.3 %collective-permute-done.37 = bf16[128,1024]{1,0:T(8,128)(2,1)S(1)} collective-permute-done((bf16[128,1024]{1,0:T(8,128)(2,1)S(1)}, bf16[128,1024]{1,0:T(8,128)(2,1)S(1)}, u32[]{:S(2)}, u32[]{:S(2)}) %collective-permute-start.37) | collective-permute-done | bytes 262176 | tf_op jit(solution)/shard_map/ppermute | solution.py:248
  436.2 23.0 %psum.7 = f32[2,512]{1,0:T(2,128)S(1)} all-reduce(f32[2,512]{1,0:T(2,128)S(1)} %pad_maximum_fusion.39), channel_id=1, replica_groups=mesh['dp'=8,'row'=2,'col'=2] {'dp'}, use_global_device_ids=true, to_apply=%region_7.9 | all-reduce | flops 1024 | bytes 8192 | tf_op jit(solution)/shard_map/psum | solution.py:407
  478.2 9.9 %collective-permute-done.62 = bf16[512,1024]{1,0:T(8,128)(2,1)} collective-permute-done((bf16[512,1024]{1,0:T(8,128)(2,1)}, bf16[512,1024]{1,0:T(8,128)(2,1)}, u32[]{:S(2)}, u32[]{:S(2)}) %collective-permute-start.62) | collective-permute-done | bytes 1048608 | tf_op jit(solution)/shard_map/ppermute | solution.py:248
  501.1 8.3 %fusion.23 = bf16[512,4096]{1,0:T(8,128)(2,1)S(1)} fusion(bf16[1024,2048]{1,0:T(8,128)(2,1)} %collective-permute-done.43, bf16[512,2048]{1,0:T(8,128)(2,1)} %collective-permute-done.42, bf16[512,2048]{1,0:T(8,128)(2,1)} %get-tuple-element.36, bf16[512,512]{1,0:T(8,128)(2,1)} %collective-permute-done.41, bf16[512,512]{1,0:T(8,128)(2,1)} %get-tuple-element.101), kind=kOutput, calls=%fused_computation.29 | convolution fusion | flops 4324327424 | bytes 13631488 | tf_op jit(solution)/shard_map/dot_general | solution.py:34
  526.8 20.0 %collective-permute-done.44 = bf16[128,4096]{1,0:T(8,128)(2,1)S(1)} collective-permute-done((bf16[128,4096]{1,0:T(8,128)(2,1)S(1)}, bf16[128,4096]{1,0:T(8,128)(2,1)S(1)}, u32[]{:S(2)}, u32[]{:S(2)}) %collective-permute-start.44) | collective-permute-done | bytes 1048608 | tf_op jit(solution)/shard_map/ppermute | solution.py:248
  549.0 16.8 %collective-permute-done.52 = bf16[128,4096]{1,0:T(8,128)(2,1)S(1)} collective-permute-done((bf16[128,4096]{1,0:T(8,128)(2,1)S(1)}, bf16[128,4096]{1,0:T(8,128)(2,1)S(1)}, u32[]{:S(2)}, u32[]{:S(2)}) %collective-permute-start.52) | collective-permute-done | bytes 1048608 | tf_op jit(solution)/shard_map/ppermute | solution.py:248
  582.1 13.6 %collective-permute-done.45 = bf16[128,4096]{1,0:T(8,128)(2,1)S(1)} collective-permute-done((bf16[128,4096]{1,0:T(8,128)(2,1)S(1)}, bf16[128,4096]{1,0:T(8,128)(2,1)S(1)}, u32[]{:S(2)}, u32[]{:S(2)}) %collective-permute-start.45) | collective-permute-done | bytes 1048608 | tf_op jit(solution)/shard_map/ppermute | solution.py:248
  599.8 18.3 %collective-permute-done.53 = bf16[128,4096]{1,0:T(8,128)(2,1)S(1)} collective-permute-done((bf16[128,4096]{1,0:T(8,128)(2,1)S(1)}, bf16[128,4096]{1,0:T(8,128)(2,1)S(1)}, u32[]{:S(2)}, u32[]{:S(2)}) %collective-permute-start.53) | collective-permute-done | bytes 1048608 | tf_op jit(solution)/shard_map/ppermute | solution.py:248
  620.8 14.2 %collective-permute-done.26 = bf16[128,3072]{1,0:T(8,128)(2,1)S(1)} collective-permute-done((bf16[128,3072]{1,0:T(8,128)(2,1)S(1)}, bf16[128,3072]{1,0:T(8,128)(2,1)S(1)}, u32[]{:S(2)}, u32[]{:S(2)}) %collective-permute-start.26) | collective-permute-done | bytes 786464 | tf_op jit(solution)/shard_map/ppermute | solution.py:248
  644.9 47.5 %collective-permute-done.27 = bf16[128,3072]{1,0:T(8,128)(2,1)S(1)} collective-permute-done((bf16[128,3072]{1,0:T(8,128)(2,1)S(1)}, bf16[128,3072]{1,0:T(8,128)(2,1)S(1)}, u32[]{:S(2)}, u32[]{:S(2)}) %collective-permute-start.27) | collective-permute-done | bytes 786464 | tf_op jit(solution)/shard_map/ppermute | solution.py:248
  696.4 18.9 %collective-permute-done.30 = bf16[128,3072]{1,0:T(8,128)(2,1)S(1)} collective-permute-done((bf16[128,3072]{1,0:T(8,128)(2,1)S(1)}, bf16[128,3072]{1,0:T(8,128)(2,1)S(1)}, u32[]{:S(2)}, u32[]{:S(2)}) %collective-permute-start.30) | collective-permute-done | bytes 786464 | tf_op jit(solution)/shard_map/ppermute | solution.py:249
  722.1 15.7 %collective-permute-done.57 = bf16[128,4096]{1,0:T(8,128)(2,1)S(1)} collective-permute-done((bf16[128,4096]{1,0:T(8,128)(2,1)S(1)}, bf16[128,4096]{1,0:T(8,128)(2,1)S(1)}, u32[]{:S(2)}, u32[]{:S(2)}) %collective-permute-start.57) | collective-permute-done | bytes 1048608 | tf_op jit(solution)/shard_map/ppermute | solution.py:249
  (368 shorter events, 291.4 us)
Async XLA Ops:
  1.4 55.1 %collective-permute-start.2 = (f32[2,512]{1,0:T(2,128)S(1)}, f32[2,512]{1,0:T(2,128)S(1)}, u32[]{:S(2)}, u32[]{:S(2)}) collective-permute-start(f32[2,512]{1,0:T(2,128)S(1)} %pad_maximum_fusion.38), channel_id=1, source_target_pairs={{0,1},{1,0},{2,3},{3,2},{4,5},{5,4},{6,7},{7,6},{8,9},{9,8},{10,11... | collective-permute-start | bytes 12296 | tf_op jit(solution)/shard_map/ppermute | solution.py:203
  17.0 77.1 %collective-permute-start.5 = (bf16[512,1024]{1,0:T(8,128)(2,1)}, bf16[512,1024]{1,0:T(8,128)(2,1)}, u32[]{:S(2)}, u32[]{:S(2)}) collective-permute-start(bf16[512,1024]{1,0:T(8,128)(2,1)} %get-tuple-element.88), channel_id=1, source_target_pairs={{0,2},{2,0},{1,3},{3,1},{4,6},{6,4},{5,7},{7,5},{8,10},{10,8},{9,1... | collective-permute-start | bytes 3145736 | tf_op jit(solution)/shard_map/ppermute | solution.py:200
  45.5 103.8 %collective-permute-start.9 = (bf16[1024,4096]{1,0:T(8,128)(2,1)}, bf16[1024,4096]{1,0:T(8,128)(2,1)}, u32[]{:S(2)}, u32[]{:S(2)}) collective-permute-start(bf16[1024,4096]{1,0:T(8,128)(2,1)} %pad_maximum_fusion.1), channel_id=1, source_target_pairs={{0,2},{2,0},{1,3},{3,1},{4,6},{6,4},{5,7},{7,5},{8,10},{10,8},{9,1... | collective-permute-start | bytes 25165832 | tf_op jit(solution)/shard_map/ppermute | solution.py:200
  140.4 233.2 %collective-permute-start.60 = (bf16[512,1024]{1,0:T(8,128)(2,1)}, bf16[512,1024]{1,0:T(8,128)(2,1)}, u32[]{:S(2)}, u32[]{:S(2)}) collective-permute-start(bf16[512,1024]{1,0:T(8,128)(2,1)} %maximum_select_fusion.3), channel_id=1, source_target_pairs={{0,4},{4,0},{8,12},{12,8},{16,20},{20,16},{24,28},{28,24},{1,5},{5... | collective-permute-start | bytes 3145736 | tf_op jit(solution)/shard_map/ppermute | solution.py:206
  226.9 80.1 %collective-permute-start.42 = (bf16[512,2048]{1,0:T(8,128)(2,1)}, bf16[512,2048]{1,0:T(8,128)(2,1)}, u32[]{:S(2)}, u32[]{:S(2)}) collective-permute-start(bf16[512,2048]{1,0:T(8,128)(2,1)} %get-tuple-element.36), channel_id=1, source_target_pairs={{0,4},{4,0},{8,12},{12,8},{16,20},{20,16},{24,28},{28,24},{1,5},{5... | collective-permute-start | bytes 6291464 | tf_op jit(solution)/shard_map/ppermute | solution.py:206
  228.2 69.9 %collective-permute-start.58 = (bf16[512,1024]{1,0:T(8,128)(2,1)S(1)}, bf16[512,1024]{1,0:T(8,128)(2,1)S(1)}, u32[]{:S(2)}, u32[]{:S(2)}) collective-permute-start(bf16[512,1024]{1,0:T(8,128)(2,1)S(1)} %get-tuple-element.62), channel_id=1, source_target_pairs={{0,4},{4,0},{8,12},{12,8},{16,20},{20,16},{24,28},{28,24},{1,5},{5... | collective-permute-start | bytes 3145736 | tf_op jit(solution)/shard_map/ppermute | solution.py:206
  250.0 49.8 %collective-permute-start.12 = (bf16[512,512]{1,0:T(8,128)(2,1)S(1)}, bf16[512,512]{1,0:T(8,128)(2,1)S(1)}, u32[]{:S(2)}, u32[]{:S(2)}) collective-permute-start(bf16[512,512]{1,0:T(8,128)(2,1)S(1)} %dynamic-slice_convert_fusion.1), channel_id=1, source_target_pairs={{0,1},{1,0},{2,3},{3,2},{4,5},{5,4},{6,7},{7,6},{8,9},{9,8},{10,11... | collective-permute-start | bytes 1572872 | tf_op jit(solution)/shard_map/ppermute | solution.py:203
  255.3 69.6 %collective-permute-start.34 = (bf16[512,1024]{1,0:T(8,128)(2,1)}, bf16[512,1024]{1,0:T(8,128)(2,1)}, u32[]{:S(2)}, u32[]{:S(2)}) collective-permute-start(bf16[512,1024]{1,0:T(8,128)(2,1)} %get-tuple-element.32), channel_id=1, source_target_pairs={{0,4},{4,0},{8,12},{12,8},{16,20},{20,16},{24,28},{28,24},{1,5},{5... | collective-permute-start | bytes 3145736 | tf_op jit(solution)/shard_map/ppermute | solution.py:206
  301.8 91.3 %all-to-all-start.1 = ((bf16[2,1,256,512]{3,0,1,2:T(2,128)(2,1)}), bf16[2,1,256,512]{3,0,1,2:T(2,128)(2,1)S(1)}, u32[]{:S(2)}, u32[]{:S(2)}) async-start(bf16[2,1,256,512]{3,0,1,2:T(2,128)(2,1)} %copy.46), calls=%async_computation.1 | async-start | bytes 1048576 | tf_op jit(solution)/shard_map/all_to_all | solution.py:416
  307.0 81.9 %collective-permute-start.50 = (bf16[512,2048]{1,0:T(8,128)(2,1)}, bf16[512,2048]{1,0:T(8,128)(2,1)}, u32[]{:S(2)}, u32[]{:S(2)}) collective-permute-start(bf16[512,2048]{1,0:T(8,128)(2,1)} %get-tuple-element.37), channel_id=1, source_target_pairs={{0,4},{4,0},{8,12},{12,8},{16,20},{20,16},{24,28},{28,24},{1,5},{5... | collective-permute-start | bytes 6291464 | tf_op jit(solution)/shard_map/ppermute | solution.py:206
  313.3 60.8 %collective-permute-start.59 = (bf16[1024,1024]{1,0:T(8,128)(2,1)}, bf16[1024,1024]{1,0:T(8,128)(2,1)}, u32[]{:S(2)}, u32[]{:S(2)}) collective-permute-start(bf16[1024,1024]{1,0:T(8,128)(2,1)} %pad_maximum_fusion.15), channel_id=1, source_target_pairs={{0,2},{2,0},{1,3},{3,1},{4,6},{6,4},{5,7},{7,5},{8,10},{10,8},{9,1... | collective-permute-start | bytes 6291464 | tf_op jit(solution)/shard_map/ppermute | solution.py:200
  325.0 174.8 %collective-permute-start.43 = (bf16[1024,2048]{1,0:T(8,128)(2,1)}, bf16[1024,2048]{1,0:T(8,128)(2,1)}, u32[]{:S(2)}, u32[]{:S(2)}) collective-permute-start(bf16[1024,2048]{1,0:T(8,128)(2,1)} %pad_maximum_fusion.8), channel_id=1, source_target_pairs={{0,2},{2,0},{1,3},{3,1},{4,6},{6,4},{5,7},{7,5},{8,10},{10,8},{9,1... | collective-permute-start | bytes 12582920 | tf_op jit(solution)/shard_map/ppermute | solution.py:200
  393.1 116.5 %collective-permute-start.51 = (bf16[1024,2048]{1,0:T(8,128)(2,1)}, bf16[1024,2048]{1,0:T(8,128)(2,1)}, u32[]{:S(2)}, u32[]{:S(2)}) collective-permute-start(bf16[1024,2048]{1,0:T(8,128)(2,1)} %pad_maximum_fusion.9), channel_id=1, source_target_pairs={{0,2},{2,0},{1,3},{3,1},{4,6},{6,4},{5,7},{7,5},{8,10},{10,8},{9,1... | collective-permute-start | bytes 12582920 | tf_op jit(solution)/shard_map/ppermute | solution.py:200
  397.3 74.7 %collective-permute-start.24 = (bf16[512,1536]{1,0:T(8,128)(2,1)}, bf16[512,1536]{1,0:T(8,128)(2,1)}, u32[]{:S(2)}, u32[]{:S(2)}) collective-permute-start(bf16[512,1536]{1,0:T(8,128)(2,1)} %constant_dynamic-update-slice_fusion), channel_id=1, source_target_pairs={{0,4},{4,0},{8,12},{12,8},{16,20},{20,16},{24,28},{28,24},{1,5},{5... | collective-permute-start | bytes 4718600 | tf_op jit(solution)/shard_map/ppermute | solution.py:206
  472.0 99.6 %collective-permute-start.23 = (bf16[512,512]{1,0:T(8,128)(2,1)}, bf16[512,512]{1,0:T(8,128)(2,1)}, u32[]{:S(2)}, u32[]{:S(2)}) collective-permute-start(bf16[512,512]{1,0:T(8,128)(2,1)} %get-tuple-element.108), channel_id=1, source_target_pairs={{0,4},{4,0},{8,12},{12,8},{16,20},{20,16},{24,28},{28,24},{1,5},{5... | collective-permute-start | bytes 1572872 | tf_op jit(solution)/shard_map/ppermute | solution.py:206
  488.1 85.4 %collective-permute-start.25 = (bf16[1024,1536]{1,0:T(8,128)(2,1)}, bf16[1024,1536]{1,0:T(8,128)(2,1)}, u32[]{:S(2)}, u32[]{:S(2)}) collective-permute-start(bf16[1024,1536]{1,0:T(8,128)(2,1)} %pad_maximum_fusion.11), channel_id=1, source_target_pairs={{0,2},{2,0},{1,3},{3,1},{4,6},{6,4},{5,7},{7,5},{8,10},{10,8},{9,1... | collective-permute-start | bytes 9437192 | tf_op jit(solution)/shard_map/ppermute | solution.py:200
  496.4 70.4 %collective-permute-start.63 = (bf16[512,1024]{1,0:T(8,128)(2,1)S(1)}, bf16[512,1024]{1,0:T(8,128)(2,1)S(1)}, u32[]{:S(2)}, u32[]{:S(2)}) collective-permute-start(bf16[512,1024]{1,0:T(8,128)(2,1)S(1)} %get-tuple-element.45), channel_id=1, source_target_pairs={{0,8},{4,12},{8,16},{12,20},{16,24},{20,28},{1,9},{5,13},{9,17},{1... | collective-permute-start | bytes 3145736 | tf_op jit(solution)/shard_map/ppermute | solution.py:248
  580.1 54.9 %collective-permute-start.26 = (bf16[128,3072]{1,0:T(8,128)(2,1)S(1)}, bf16[128,3072]{1,0:T(8,128)(2,1)S(1)}, u32[]{:S(2)}, u32[]{:S(2)}) collective-permute-start(bf16[128,3072]{1,0:T(8,128)(2,1)S(1)} %get-tuple-element.59), channel_id=1, source_target_pairs={{0,8},{4,12},{1,9},{5,13},{2,10},{6,14},{3,11},{7,15}} | collective-permute-start | bytes 2359304 | tf_op jit(solution)/shard_map/ppermute | solution.py:248
  581.4 61.6 %collective-permute-start.29 = (bf16[128,3072]{1,0:T(8,128)(2,1)S(1)}, bf16[128,3072]{1,0:T(8,128)(2,1)S(1)}, u32[]{:S(2)}, u32[]{:S(2)}) collective-permute-start(bf16[128,3072]{1,0:T(8,128)(2,1)S(1)} %get-tuple-element.60), channel_id=1, source_target_pairs={{28,20},{24,16},{29,21},{25,17},{30,22},{26,18},{31,23},{27,19}} | collective-permute-start | bytes 2359304 | tf_op jit(solution)/shard_map/ppermute | solution.py:249
  596.4 121.0 %collective-permute-start.46 = (bf16[128,4096]{1,0:T(8,128)(2,1)S(1)}, bf16[128,4096]{1,0:T(8,128)(2,1)S(1)}, u32[]{:S(2)}, u32[]{:S(2)}) collective-permute-start(bf16[128,4096]{1,0:T(8,128)(2,1)S(1)} %get-tuple-element.53), channel_id=1, source_target_pairs={{0,8},{4,12},{8,16},{12,20},{16,24},{20,28},{1,9},{5,13},{9,17},{1... | collective-permute-start | bytes 3145736 | tf_op jit(solution)/shard_map/ppermute | solution.py:248
  618.9 103.2 %collective-permute-start.54 = (bf16[128,4096]{1,0:T(8,128)(2,1)S(1)}, bf16[128,4096]{1,0:T(8,128)(2,1)S(1)}, u32[]{:S(2)}, u32[]{:S(2)}) collective-permute-start(bf16[128,4096]{1,0:T(8,128)(2,1)S(1)} %get-tuple-element.49), channel_id=1, source_target_pairs={{0,8},{4,12},{8,16},{12,20},{16,24},{20,28},{1,9},{5,13},{9,17},{1... | collective-permute-start | bytes 3145736 | tf_op jit(solution)/shard_map/ppermute | solution.py:248
  635.0 59.2 %collective-permute-start.56 = (bf16[128,4096]{1,0:T(8,128)(2,1)S(1)}, bf16[128,4096]{1,0:T(8,128)(2,1)S(1)}, u32[]{:S(2)}, u32[]{:S(2)}) collective-permute-start(bf16[128,4096]{1,0:T(8,128)(2,1)S(1)} %get-tuple-element.50), channel_id=1, source_target_pairs={{28,20},{24,16},{20,12},{16,8},{29,21},{25,17},{21,13},{17,9},{30,... | collective-permute-start | bytes 3145736 | tf_op jit(solution)/shard_map/ppermute | solution.py:249
  636.5 55.9 %collective-permute-start.27 = (bf16[128,3072]{1,0:T(8,128)(2,1)S(1)}, bf16[128,3072]{1,0:T(8,128)(2,1)S(1)}, u32[]{:S(2)}, u32[]{:S(2)}) collective-permute-start(bf16[128,3072]{1,0:T(8,128)(2,1)S(1)} %add_convert_fusion.15), channel_id=1, source_target_pairs={{0,8},{4,12},{8,16},{12,20},{1,9},{5,13},{9,17},{13,21},{2,10},{6,... | collective-permute-start | bytes 2359304 | tf_op jit(solution)/shard_map/ppermute | solution.py:248
  643.0 78.4 %collective-permute-start.49 = (bf16[128,4096]{1,0:T(8,128)(2,1)S(1)}, bf16[128,4096]{1,0:T(8,128)(2,1)S(1)}, u32[]{:S(2)}, u32[]{:S(2)}) collective-permute-start(bf16[128,4096]{1,0:T(8,128)(2,1)S(1)} %add_convert_fusion.8), channel_id=1, source_target_pairs={{28,20},{24,16},{20,12},{16,8},{12,4},{8,0},{29,21},{25,17},{21,13... | collective-permute-start | bytes 3145736 | tf_op jit(solution)/shard_map/ppermute | solution.py:249
  (100 other events, 1848.9 us)

commit v2 on v1

v2 whole, which is shorter than its diff:
```python
import math

import jax
import jax.numpy as jnp
from jax import lax
from jax.experimental import pallas as pl
from jax.experimental.pallas import tpu as pltpu
from jax.sharding import PartitionSpec as P

D = 2048
HEADS = 32
HEAD_DIM = 64
SL = 256
MICRO = 2
ROWS = MICRO * SL

EPSILON = 1e-05
ROPE_THETA = 130000.0
MASKED_SCORE = -1000000000.0
F32 = jnp.float32
BF16 = jnp.bfloat16
SWAP = [(0, 1), (1, 0)]


def mm(a, b):
    return jnp.dot(a, b, preferred_element_type=F32)


def mm_nt(a, b):
    return lax.dot_general(a, b, (((1,), (1,)), ((), ())), preferred_element_type=F32)


def mm_tn(a, b):
    return lax.dot_general(a, b, (((0,), (0,)), ((), ())), preferred_element_type=F32)


def rope_tables():
    half = HEAD_DIM // 2
    frequency = jnp.exp(
        jnp.arange(half, dtype=F32) * (-2.0 * math.log(ROPE_THETA) / HEAD_DIM)
    )
    angles = jnp.arange(SL, dtype=F32)[:, None] * frequency[None, :]
    cosine = jnp.cos(angles)
    sine = jnp.sin(angles)
    zero = jnp.zeros_like(sine)
    table_cos = jnp.concatenate([cosine] * 4, axis=1)
    table_first = jnp.concatenate([sine, zero] * 2, axis=1)
    table_second = jnp.concatenate([zero, sine] * 2, axis=1)
    return table_cos, table_first, table_second


def turn(v, cos, first, second):
    ahead = pltpu.roll(v, 128 - HEAD_DIM // 2, 1)
    behind = pltpu.roll(v, HEAD_DIM // 2, 1)
    return v * cos - ahead * first + behind * second


def turn_back(v, cos, first, second):
    ahead = pltpu.roll(v, 128 - HEAD_DIM // 2, 1)
    behind = pltpu.roll(v, HEAD_DIM // 2, 1)
    return v * cos + ahead * first - behind * second


def head_mask(head):
    lane = lax.broadcasted_iota(jnp.int32, (SL, 128), 1)
    return (lane // HEAD_DIM) == head


def softmax_of(q, k, allowed):
    scores = mm_nt(q, k) * HEAD_DIM ** (-0.5)
    scores = jnp.where(allowed, scores, MASKED_SCORE)
    exps = jnp.exp(scores - jnp.max(scores, axis=1, keepdims=True))
    return exps / jnp.sum(exps, axis=1, keepdims=True)


def allowed_of(length):
    query = lax.broadcasted_iota(jnp.int32, (SL, SL), 0)
    key = lax.broadcasted_iota(jnp.int32, (SL, SL), 1)
    return (key <= query) & (key < length)


FREE = pl.CostEstimate(flops=0, bytes_accessed=0, transcendentals=0)
BUSY = pl.CostEstimate(flops=20 * 10**9, bytes_accessed=60 * 10**6, transcendentals=0)


def whole(shape):
    return pl.BlockSpec(shape, lambda *at: (0,) * len(shape), pipeline_mode=pl.Buffered(1))


def attend_kernel(len_ref, qkv_ref, cos_ref, first_ref, second_ref, o_ref, turned_ref):
    cos, first, second = cos_ref[...], first_ref[...], second_ref[...]
    qr = turn(qkv_ref[:, :128], cos, first, second).astype(BF16)
    kr = turn(qkv_ref[:, 128:256], cos, first, second).astype(BF16)
    vr = qkv_ref[:, 256:].astype(BF16)
    turned_ref[:, :128] = qr
    turned_ref[:, 128:256] = kr
    turned_ref[:, 256:] = vr
    allowed = allowed_of(len_ref[pl.program_id(0)])
    out = jnp.zeros((SL, 128), F32)
    for head in range(2):
        mask = head_mask(head)
        probs = softmax_of(jnp.where(mask, qr, jnp.zeros_like(qr)), kr, allowed).astype(BF16)
        out = out + mm(probs, jnp.where(mask, vr, jnp.zeros_like(vr)))
    o_ref[...] = out.astype(BF16)


def attend_grad_kernel(len_ref, turned_ref, od_ref, cos_ref, first_ref, second_ref, grad_ref):
    cos, first, second = cos_ref[...], first_ref[...], second_ref[...]
    qr, kr, vr = turned_ref[:, :128], turned_ref[:, 128:256], turned_ref[:, 256:]
    od = od_ref[...]
    allowed = allowed_of(len_ref[pl.program_id(0)])
    dq = jnp.zeros((SL, 128), F32)
    dk = jnp.zeros((SL, 128), F32)
    dv = jnp.zeros((SL, 128), F32)
    zero = jnp.zeros_like(qr)
    for head in range(2):
        mask = head_mask(head)
        q_own = jnp.where(mask, qr, zero)
        k_own = jnp.where(mask, kr, zero)
        od_own = jnp.where(mask, od, zero)
        probs = softmax_of(q_own, kr, allowed)
        d_probs = mm_nt(od_own, vr)
        dv = dv + mm_tn(probs.astype(BF16), od_own)
        inner = jnp.sum(probs * d_probs, axis=1, keepdims=True)
        d_scores = (probs * (d_probs - inner)).astype(BF16)
        dq = dq + mm(d_scores, k_own)
        dk = dk + mm_tn(d_scores, q_own)
    scale = HEAD_DIM ** (-0.5)
    grad_ref[:, :128] = turn_back(dq * scale, cos, first, second).astype(BF16)
    grad_ref[:, 128:256] = turn_back(dk * scale, cos, first, second).astype(BF16)
    grad_ref[:, 256:] = dv.astype(BF16)


def pair_block(width):
    return pl.BlockSpec((SL, width), lambda m, h, lens: (m, h))


TABLE = pl.BlockSpec((SL, 128), lambda m, h, lens: (0, 0))


def attend_forward(lengths, qkv, tables):
    width = qkv.shape[1]
    return pl.pallas_call(
        attend_kernel,
        out_shape=(
            jax.ShapeDtypeStruct((ROWS, width // 3), BF16),
            jax.ShapeDtypeStruct((ROWS, width), BF16),
        ),
        grid_spec=pltpu.PrefetchScalarGridSpec(
            num_scalar_prefetch=1,
            grid=(MICRO, width // 384),
            in_specs=[pair_block(384)] + [TABLE] * 3,
            out_specs=[pair_block(128), pair_block(384)],
        ),
        cost_estimate=FREE,
    )(lengths, qkv, *tables)


def attend_backward(lengths, turned, od, tables):
    width = turned.shape[1]
    return pl.pallas_call(
        attend_grad_kernel,
        out_shape=jax.ShapeDtypeStruct((ROWS, width), BF16),
        grid_spec=pltpu.PrefetchScalarGridSpec(
            num_scalar_prefetch=1,
            grid=(MICRO, width // 384),
            in_specs=[pair_block(384), pair_block(128)] + [TABLE] * 3,
            out_specs=pair_block(384),
        ),
        cost_estimate=FREE,
    )(lengths, turned, od, *tables)


def multiply(a, w, transposed, tile, dtype):
    height, depth = a.shape
    width = w.shape[0] if transposed else w.shape[1]

    def kernel(a_ref, w_ref, o_ref):
        form = mm_nt if transposed else mm
        o_ref[...] = form(a_ref[...], w_ref[...]).astype(dtype)

    if transposed:
        w_spec = pl.BlockSpec((tile, depth), lambda j: (j, 0))
    else:
        w_spec = pl.BlockSpec((depth, tile), lambda j: (0, j))
    return pl.pallas_call(
        kernel,
        out_shape=jax.ShapeDtypeStruct((height, width), dtype),
        grid=(width // tile,),
        in_specs=[whole(a.shape), w_spec],
        out_specs=pl.BlockSpec((height, tile), lambda j: (0, j)),
        cost_estimate=FREE,
    )(a, w)


def split_product(parts, w, transposed, tile, cost=FREE):
    count = len(parts)
    height = parts[0].shape[0]
    width = w.shape[0] if transposed else w.shape[1]
    steps = width // tile
    half = steps // 2

    def kernel(*refs):
        form = mm_nt if transposed else mm
        total = form(refs[0][...], refs[count][...])
        for at in range(1, count):
            total = total + form(refs[at][...], refs[count + at][...])
        kept_ref, sent_ref = refs[2 * count :]
        step = pl.program_id(0)

        @pl.when(step < half)
        def _():
            sent_ref[...] = total.astype(BF16)

        @pl.when(step >= half)
        def _():
            kept_ref[...] = total

    def w_spec(at, depth):
        if transposed:
            return pl.BlockSpec((tile, depth), lambda j: (lax.rem(j + half, steps), at))
        return pl.BlockSpec((depth, tile), lambda j: (at, lax.rem(j + half, steps)))

    return pl.pallas_call(
        kernel,
        out_shape=(
            jax.ShapeDtypeStruct((height, width // 2), F32),
            jax.ShapeDtypeStruct((height, width // 2), BF16),
        ),
        grid=(steps,),
        in_specs=[whole(part.shape) for part in parts]
        + [w_spec(at, part.shape[1]) for at, part in enumerate(parts)],
        out_specs=(
            pl.BlockSpec((height, tile), lambda j: (0, jnp.maximum(j - half, 0))),
            pl.BlockSpec((height, tile), lambda j: (0, jnp.minimum(j, half - 1))),
        ),
        cost_estimate=cost,
    )(*parts, *([w] * count))


def feed_kernel(x_ref, gate_ref, up_ref, da_ref, hidden_ref, dg_ref, du_ref):
    x = x_ref[...]
    gate = mm(x, gate_ref[...])
    up = mm(x, up_ref[...])
    da = da_ref[...]
    sigmoid = 1.0 / (1.0 + jnp.exp(-gate))
    swish = gate * sigmoid
    hidden_ref[...] = (swish * up).astype(BF16)
    dg_ref[...] = (da * up * sigmoid * (1.0 + gate * (1.0 - sigmoid))).astype(BF16)
    du_ref[...] = (da * swish).astype(BF16)


def feed_forward(x, pair_w, hidden_grad, tile=256):
    height, depth = x.shape
    width = hidden_grad.shape[1]
    steps = width // tile
    tall = pl.BlockSpec((height, tile), lambda j: (0, j))
    return pl.pallas_call(
        feed_kernel,
        out_shape=(jax.ShapeDtypeStruct((height, width), BF16),) * 3,
        grid=(steps,),
        in_specs=[
            whole(x.shape),
            pl.BlockSpec((depth, tile), lambda j: (0, j)),
            pl.BlockSpec((depth, tile), lambda j: (0, j + steps)),
            tall,
        ],
        out_specs=(tall,) * 3,
        cost_estimate=FREE,
    )(x, pair_w, pair_w, hidden_grad)


def side_grads(left, left_across, right):
    depth, height = left[0].shape
    width = right[0].shape[1]
    tile = width // 2

    def kernel(lo, lr, xo, xr, ro, rr, o_ref):
        @pl.when(pl.program_id(0) == 0)
        def _():
            o_ref[...] = (mm_tn(lo[...], ro[...]) + mm_tn(lr[...], rr[...])).astype(BF16)

        @pl.when(pl.program_id(0) == 1)
        def _():
            o_ref[...] = (mm_tn(xo[...], ro[...]) + mm_tn(xr[...], rr[...])).astype(BF16)

    wide = pl.BlockSpec((depth, tile), lambda p, j: (0, j))
    return pl.pallas_call(
        kernel,
        out_shape=jax.ShapeDtypeStruct((2 * height, width), BF16),
        grid=(2, 2),
        in_specs=[whole(left[0].shape)] * 4 + [wide] * 2,
        out_specs=pl.BlockSpec((height, tile), lambda p, j: (p, j)),
        cost_estimate=FREE,
    )(*left, *left_across, *right)


def wide_grads(left, right, right_across):
    depth, height = left[0].shape
    width = right[0].shape[1]
    tile = width // 2

    def kernel(lo, lr, ro, rr, xo, xr, o_ref):
        @pl.when(pl.program_id(0) == 0)
        def _():
            o_ref[...] = (mm_tn(lo[...], ro[...]) + mm_tn(lr[...], rr[...])).astype(BF16)

        @pl.when(pl.program_id(0) == 1)
        def _():
            o_ref[...] = (mm_tn(lo[...], xo[...]) + mm_tn(lr[...], xr[...])).astype(BF16)

    own = pl.BlockSpec((depth, tile), lambda p, j: (0, jnp.where(p == 0, j, 1)))
    across = pl.BlockSpec((depth, tile), lambda p, j: (0, jnp.where(p == 0, 0, j)))
    return pl.pallas_call(
        kernel,
        out_shape=jax.ShapeDtypeStruct((height, 2 * width), BF16),
        grid=(2, 2),
        in_specs=[whole(left[0].shape)] * 2 + [own] * 2 + [across] * 2,
        out_specs=pl.BlockSpec((height, tile), lambda p, j: (0, 2 * p + j)),
        cost_estimate=FREE,
    )(*left, *right, *right_across)


def line_add_kernel(at_ref, gr_ref, gl_ref, r_ref, l_ref, right_ref, left_ref):
    right_ref[...] = (gr_ref[...].astype(F32) + r_ref[...].astype(F32)).astype(BF16)
    left_ref[...] = (gl_ref[...].astype(F32) + l_ref[...].astype(F32)).astype(BF16)


def line_add(at, grads, right, left):
    height, width = right.shape
    tile = width // 4
    plain = pl.BlockSpec((height, tile), lambda j, at: (0, j))
    shape = jax.ShapeDtypeStruct(right.shape, BF16)
    return pl.pallas_call(
        line_add_kernel,
        out_shape=(shape, shape),
        grid_spec=pltpu.PrefetchScalarGridSpec(
            num_scalar_prefetch=1,
            grid=(4,),
            in_specs=[
                pl.BlockSpec((height, tile), lambda j, at: (at[0], j)),
                pl.BlockSpec((height, tile), lambda j, at: (at[1], j)),
                plain,
                plain,
            ],
            out_specs=[plain, plain],
        ),
        cost_estimate=FREE,
    )(at, grads, grads, right, left)


def line_end_kernel(pieces, at_ref, g_ref, r_ref, l_ref, *out_refs):
    total = g_ref[...].astype(F32) + r_ref[...].astype(F32) + l_ref[...].astype(F32)
    size = total.shape[1] // pieces
    for k in range(pieces):
        out_refs[k][...] = total[:, k * size : (k + 1) * size]


def line_end(at, grads, right, left, pieces, parts, tiles):
    height, width = right.shape
    tile = width // (parts * tiles)

    def came(p, j, at):
        return (0, p * tiles + j)

    def out(p, j, at):
        return (0, jnp.where(at[1] == 0, p, parts - 1 - p) * tiles + j)

    return pl.pallas_call(
        lambda *refs: line_end_kernel(pieces, *refs),
        out_shape=(jax.ShapeDtypeStruct((height, width // pieces), F32),) * pieces,
        grid_spec=pltpu.PrefetchScalarGridSpec(
            num_scalar_prefetch=1,
            grid=(parts, tiles),
            in_specs=[
                pl.BlockSpec((height, tile), lambda p, j, at: (at[0], p * tiles + j)),
                pl.BlockSpec((height, tile), came),
                pl.BlockSpec((height, tile), came),
            ],
            out_specs=[pl.BlockSpec((height, tile // pieces), out)] * pieces,
        ),
        cost_estimate=FREE,
    )(at, grads, right, left)


def swap_kernel(plan, given, count, *refs):
    weights, outs = refs[:given], refs[given : given + count]
    rest = refs[given + count :]
    held, (send_sem, recv_sem, in_sem, out_sem) = rest[: len(plan)], rest[len(plan) :]
    row = lax.axis_index("row")
    barrier = pltpu.get_barrier_semaphore()
    pl.semaphore_signal(
        barrier, inc=1, device_id={"row": 1 - row}, device_id_type=pl.DeviceIdType.MESH
    )
    remote, local = [], []
    for at, (source, by_rows, out, start, offset, size) in enumerate(plan):
        weight = weights[source]
        height, width = weight.shape

        def part(index):
            if by_rows:
                return weight.at[pl.ds(pl.multiple_of(index * size, size), size), :]
            first = pl.multiple_of(index * (width // 2) + start, 128)
            return weight.at[:, pl.ds(first, size)]

        def place(second):
            if by_rows:
                return outs[out].at[:, pl.ds(second * width, width)]
            return outs[out].at[pl.ds(second * height, height), pl.ds(offset, size)]

        remote.append(
            pltpu.make_async_remote_copy(
                src_ref=part(1 - row),
                dst_ref=place(1),
                send_sem=send_sem.at[at],
                recv_sem=recv_sem.at[at],
                device_id={"row": 1 - row},
                device_id_type=pl.DeviceIdType.MESH,
            )
        )
        local.append(
            (
                pltpu.make_async_copy(part(row), held[at], in_sem.at[at]),
                pltpu.make_async_copy(held[at], place(0), out_sem.at[at]),
            )
        )
    for fetch, _ in local:
        fetch.start()
    pl.semaphore_wait(barrier, 1)
    for copy in remote:
        copy.start()
    for fetch, store in local:
        fetch.wait()
        store.start()
    for _, store in local:
        store.wait()
    for copy in remote:
        copy.wait()


def swap_weights(weights, plan, shapes, identity):
    held = []
    for source, by_rows, _, _, _, size in plan:
        height, width = weights[source].shape
        held.append((size, width) if by_rows else (height, size))
    sems = pltpu.SemaphoreType.DMA((len(plan),))
    return pl.pallas_call(
        lambda *refs: swap_kernel(plan, len(weights), len(shapes), *refs),
        out_shape=[jax.ShapeDtypeStruct(shape, BF16) for shape in shapes],
        in_specs=[pl.BlockSpec(memory_space=pl.ANY)] * len(weights),
        out_specs=[pl.BlockSpec(memory_space=pl.ANY)] * len(shapes),
        scratch_shapes=[pltpu.VMEM(shape, BF16) for shape in held] + [sems] * 4,
        compiler_params=pltpu.CompilerParams(collective_id=identity, has_side_effects=True),
        cost_estimate=FREE,
    )(*weights)


MESH = pl.DeviceIdType.MESH


def greet(*moves):
    barrier = pltpu.get_barrier_semaphore()
    total = 0
    for count, target in moves:
        total = total + count

        @pl.when(count > 0)
        def _():
            pl.semaphore_signal(barrier, inc=1, device_id=target, device_id_type=MESH)

    pl.semaphore_wait(barrier, total)


class ZLine:
    def __init__(self, line, grads, out, stage, came, sems, count, sided):
        self.line, self.grads, self.out, self.stage = line, grads, out, stage
        self.came, self.sems, self.sided = came, sems, sided
        width = grads.shape[1] // count
        self.pieces = [(k, pl.ds(k * width, width)) for k in range(count)]
        self.dp, self.row = lax.axis_index("dp"), lax.axis_index("row")
        self.z = self.dp // 2
        self.last = line - 1
        self.ways = ((0, self.z, 2), (1, self.last - self.z, -2))

    def rows_of(self, dest):
        size = self.grads.shape[0] // self.line
        if self.sided:
            dest = lax.rem(dest + self.line - self.row * (self.line // 2), self.line)
        return pl.ds(pl.multiple_of(dest * size, size), size)

    def copy(self, source, way, step, slot, piece, columns):
        return pltpu.make_async_remote_copy(
            src_ref=source,
            dst_ref=self.came.at[way, slot, :, columns],
            send_sem=self.sems.at[0, way, slot, piece],
            recv_sem=self.sems.at[1, way, slot, piece],
            device_id={"dp": self.dp + step},
            device_id_type=MESH,
        )

    def arrived(self, way, step, slot, piece, columns):
        held = self.came.at[way, slot, :, columns]
        self.copy(held, way, step, slot, piece, columns).wait_recv()
        return held

    def run(self, start, stop):
        def one_step(slot, _):
            for piece, columns in self.pieces:
                for way, place, step in self.ways:
                    far = self.last - slot + place
                    dest = far if step > 0 else self.last - far

                    @pl.when((place == 0) & (place < self.last))
                    def _():
                        source = self.grads.at[self.rows_of(dest), columns]
                        self.copy(source, way, step, slot, piece, columns).start()

                    @pl.when((place > 0) & (place <= slot))
                    def _():
                        held = self.arrived(way, step, slot - 1, piece, columns)

                        @pl.when(place < self.last)
                        def _():
                            held[...] = (
                                held[...].astype(F32)
                                + self.grads[self.rows_of(dest), columns].astype(F32)
                            ).astype(BF16)
                            self.copy(held, way, step, slot, piece, columns).start()

            return 0

        lax.fori_loop(start, stop, one_step, 0)

    def finish(self):
        own = self.rows_of(self.z)
        for piece, columns in self.pieces:
            self.stage[:, columns] = self.grads[own, columns].astype(F32)
            for way, place, step in self.ways:

                @pl.when(place > 0)
                def _():
                    held = self.arrived(way, step, self.last - 1, piece, columns)
                    self.stage[:, columns] += held[...].astype(F32)

        def settle(slot, _):
            for piece, columns in self.pieces:
                for way, place, step in self.ways:

                    @pl.when((place <= slot) & (place < self.last))
                    def _():
                        held = self.came.at[way, slot, :, columns]
                        self.copy(held, way, step, slot, piece, columns).wait_send()

            return 0

        lax.fori_loop(0, self.last, settle, 0)

    def moves(self):
        return (
            (jnp.minimum(self.z, 1), {"dp": self.dp - 2}),
            (jnp.minimum(self.last - self.z, 1), {"dp": self.dp + 2}),
        )


def tiles_loop(width, tile, body):
    def one(j, _):
        body(pl.ds(pl.multiple_of(j * tile, tile), tile), j * tile)
        return 0

    lax.fori_loop(0, width // tile, one, 0)


def tail_kernel(
    line,
    gate_grads,
    up,
    up_row,
    second_mine,
    second_came,
    dqkv,
    dqkv_row,
    first_mine,
    first_came,
    branch,
    mixed_mine,
    mixed_came,
    mixed_row,
    mixed_came_row,
    gate_out,
    up_out,
    qkv_out,
    output_out,
    gate_z,
    up_z,
    qkv_z,
    output_z,
    up_grads,
    qkv_grads,
    output_grads,
    up_came,
    up_came_row,
    dqkv_came,
    dqkv_came_row,
    branch_came,
    turned_left,
    gate_stage,
    up_stage,
    qkv_stage,
    output_stage,
    gate_sems,
    up_sems,
    qkv_sems,
    output_sems,
    swap_sems,
    out_sems,
):
    dp, row = lax.axis_index("dp"), lax.axis_index("row")
    partner = dp + 1 - 2 * lax.rem(dp, 2)
    gate_line = ZLine(line, gate_grads, gate_out, gate_stage, gate_z, gate_sems, 4, False)
    up_line = ZLine(line, up_grads, up_out, up_stage, up_z, up_sems, 4, False)
    qkv_line = ZLine(line, qkv_grads, qkv_out, qkv_stage, qkv_z, qkv_sems, 3, False)
    output_line = ZLine(line, output_grads, output_out, output_stage, output_z, output_sems, 1, True)

    def swap(source, target, at, device):
        return pltpu.make_async_remote_copy(
            src_ref=source,
            dst_ref=target,
            send_sem=swap_sems.at[0, at],
            recv_sem=swap_sems.at[1, at],
            device_id=device,
            device_id_type=MESH,
        )

    up_x = swap(up, up_came, 0, {"dp": partner})
    branch_x = swap(branch, branch_came, 1, {"dp": partner})
    dqkv_x = swap(dqkv, dqkv_came, 2, {"dp": partner})
    up_across = swap(up_came, up_came_row, 3, {"row": 1 - row})
    dqkv_across = swap(dqkv_came, dqkv_came_row, 4, {"row": 1 - row})

    def store(line_of, at):
        copy = pltpu.make_async_copy(line_of.stage, line_of.out, out_sems.at[at])
        copy.start()
        return copy

    greet(*gate_line.moves(), (jnp.int32(1), {"dp": partner}), (jnp.int32(1), {"row": 1 - row}))
    gate_line.run(0, 1)
    up_x.start()
    branch_x.start()
    dqkv_x.start()

    depth = second_mine.shape[0]
    turned_left[:, :depth] = second_mine[...].T
    turned_left[:, depth:] = second_came[...].T
    gate_line.run(1, 2)

    def wide(target, shift, mine, came):
        def body(columns, start):
            total = mm(turned_left[:, :depth], mine[:, columns])
            total = total + mm(turned_left[:, depth:], came[:, columns])
            tile = total.shape[1]
            target[:, pl.ds(pl.multiple_of(shift + start, tile), tile)] = total.astype(BF16)

        tiles_loop(mine.shape[1], 512, body)

    up_x.wait_recv()
    up_across.start()
    gate_line.run(2, line - 1)
    wide(up_grads, 0, up, up_came)
    up_across.wait_recv()
    wide(up_grads, up.shape[1], up_row, up_came_row)
    up_line.run(0, 1)
    gate_line.finish()
    gate_store = store(gate_line, 0)

    turned_left[:, :depth] = first_mine[...].T
    turned_left[:, depth:] = first_came[...].T
    branch_x.wait_recv()

    def side(start, mine, came):
        def body(columns, _):
            total = mm_tn(mine[...], branch[:, columns]) + mm_tn(came[...], branch_came[:, columns])
            output_grads[pl.ds(start, mine.shape[1]), columns] = total.astype(BF16)

        tiles_loop(branch.shape[1], 512, body)

    side(0, mixed_mine, mixed_came)
    side(mixed_mine.shape[1], mixed_row, mixed_came_row)
    output_line.run(0, 1)
    up_line.run(1, 2)
    dqkv_x.wait_recv()
    dqkv_across.start()
    wide(qkv_grads, 0, dqkv, dqkv_came)
    dqkv_across.wait_recv()
    wide(qkv_grads, dqkv.shape[1], dqkv_row, dqkv_came_row)
    qkv_line.run(0, 1)
    output_line.run(1, 2)
    up_line.run(2, line - 1)
    qkv_line.run(1, 2)
    output_line.run(2, line - 1)
    up_line.finish()
    up_store = store(up_line, 1)
    qkv_line.run(2, line - 1)
    output_line.finish()
    output_store = store(output_line, 2)
    qkv_line.finish()
    qkv_store = store(qkv_line, 3)
    for copy in (up_x, branch_x, dqkv_x, up_across, dqkv_across):
        copy.wait_send()
    for copy in (gate_store, up_store, output_store, qkv_store):
        copy.wait()


def tail_sums(line, identity, *values):
    (gate_grads, up, _, _, _, dqkv, _, _, _, branch) = values[:10]
    rows = gate_grads.shape[0]
    side_rows = 2 * values[10].shape[1]
    tokens = up.shape[0]
    widths = (gate_grads.shape[1], gate_grads.shape[1], 2 * dqkv.shape[1], branch.shape[1])
    heights = (rows, rows, rows, side_rows)
    pieces = (4, 4, 3, 1)
    sizes = [(h // line, w) for h, w in zip(heights, widths)]
    vmem = pl.BlockSpec(memory_space=pltpu.VMEM)

    def buffer(*shape):
        return pltpu.VMEM(shape, BF16)

    return pl.pallas_call(
        lambda *refs: tail_kernel(line, *refs),
        out_shape=[jax.ShapeDtypeStruct(size, F32) for size in sizes],
        in_specs=[vmem] * len(values),
        out_specs=[pl.BlockSpec(memory_space=pl.ANY)] * 4,
        scratch_shapes=[buffer(2, line - 1, *size) for size in sizes]
        + [buffer(h, w) for h, w in zip(heights[1:], widths[1:])]
        + [buffer(*up.shape)] * 2
        + [buffer(*dqkv.shape)] * 2
        + [buffer(*branch.shape)]
        + [buffer(rows, 2 * tokens)]
        + [pltpu.VMEM(size, F32) for size in sizes]
        + [pltpu.SemaphoreType.DMA((2, 2, line - 1, count)) for count in pieces]
        + [pltpu.SemaphoreType.DMA((2, 5)), pltpu.SemaphoreType.DMA((4,))],
        compiler_params=pltpu.CompilerParams(
            collective_id=identity, has_side_effects=True, vmem_limit_bytes=67043328
        ),
        cost_estimate=FREE,
    )(*values)


def per_device(
    tokens,
    lengths,
    deal_order,
    attention_gain,
    query_weight,
    key_weight,
    value_weight,
    output_weight,
    feed_gain,
    gate_weight,
    up_weight,
    down_weight,
    cotangent,
):
    groups = lax.axis_size("dp")
    line = groups // 2
    dp = lax.axis_index("dp")
    row = lax.axis_index("row")
    col = lax.axis_index("col")
    z, x = dp // 2, dp % 2
    half = D // 2
    block = D // 4

    def over_row(v):
        return lax.ppermute(v, "row", SWAP)

    def over_col(v):
        return lax.ppermute(v, "col", SWAP)

    def over_x(v):
        return lax.ppermute(v, "dp", [(i, i ^ 1) for i in range(groups)])

    def ordered(own, other, index, axis=-1):
        return jnp.where(
            index == 0,
            jnp.concatenate([own, other], axis=axis),
            jnp.concatenate([other, own], axis=axis),
        )

    def x_parts(v, width):
        even = jnp.concatenate(
            [v[:, s : s + width] for s in range(0, v.shape[1], 2 * width)], axis=1
        )
        odd = jnp.concatenate(
            [v[:, s : s + width] for s in range(width, v.shape[1], 2 * width)], axis=1
        )
        return jnp.where(x == 0, even, odd), jnp.where(x == 0, odd, even)

    token = []

    def ordered_after(*values):
        out = lax.optimization_barrier(tuple(values) + tuple(token))
        return out[: len(values)] if len(values) > 1 else out[0]

    def mark(value):
        token[:] = [value]
        return value

    def arrive(*values):
        out = ordered_after(*values)
        mark(out[0] if len(values) > 1 else out)
        return out

    class Line:
        def __init__(self, grads, index_of):
            self.grads = grads
            self.size = grads.shape[0] // line
            self.index_of = index_of
            self.step = 0
            self.right = self.left = None

        def chunk(self, at):
            return lax.dynamic_slice_in_dim(self.grads, at * self.size, self.size, 0)

        def advance(self):
            step = self.step
            if step >= line - 1:
                return
            self.step += 1
            at_right = self.index_of(jnp.clip(line - 1 - step + z, 0, line - 1))
            at_left = self.index_of(jnp.clip(step - (line - 1 - z), 0, line - 1))
            if step:
                right, left = arrive(self.right, self.left)
                send_right, send_left = line_add(
                    jnp.stack([at_right, at_left]), self.grads, right, left
                )
                mark(send_left)
            else:
                send_right, send_left = self.chunk(at_right), self.chunk(at_left)
            rights = [
                (2 * i + k, 2 * i + 2 + k) for i in range(min(step, line - 2) + 1) for k in range(2)
            ]
            lefts = [(2 * (line - 1) + 1 - a, 2 * (line - 1) + 1 - b) for a, b in rights]
            self.right = lax.ppermute(send_right, "dp", rights)
            self.left = lax.ppermute(send_left, "dp", lefts)

        def total(self, pieces, parts, tiles):
            while self.step < line - 1:
                self.advance()
            right, left = arrive(self.right, self.left)
            at = jnp.stack([self.index_of(z), row])
            out = line_end(at, self.grads, right, left, pieces, parts, tiles)
            mark(out[0])
            return out

    def plain_index(dest):
        return dest

    def side_index(dest):
        return lax.rem(dest + line - row * (line // 2), line)

    def all_sum(v):
        if groups & (groups - 1):
            return lax.psum(v, "dp")
        reach = 1
        while reach < groups:
            v = v + lax.ppermute(v, "dp", [(i, i ^ reach) for i in range(groups)])
            reach *= 2
        return v

    gathered = jnp.take_along_axis(tokens, deal_order[:, :, None, None], axis=1)
    gathered = mark(lax.optimization_barrier(gathered))
    dealt = lax.all_to_all(gathered, "dp", split_axis=1, concat_axis=2, tiled=True)
    own_order = lax.dynamic_slice_in_dim(deal_order, dp, 1, 1)
    own_lengths = jnp.take_along_axis(lengths, own_order, axis=1)[:, 0]
    tables = rope_tables()
    live = (jnp.arange(SL, dtype=jnp.int32)[None, :] < own_lengths[:, None]).reshape(ROWS, 1)
    top_block = jnp.where(live, cotangent.reshape(ROWS, block), 0.0).astype(BF16)

    gains = jnp.stack([attention_gain, feed_gain])
    gains_half = ordered(gains, over_col(gains), col)
    gains_other = over_row(gains_half)
    gains_full = jnp.concatenate([gains_half, gains_other], axis=1)

    top_col = over_col(top_block)
    quarter = gate_weight.shape[1] // 2
    gate_weight, up_weight = ordered_after(gate_weight, up_weight)
    (pair_w,) = swap_weights(
        (gate_weight, up_weight),
        ((0, False, 0, 0, 0, quarter), (1, False, 0, 0, quarter, quarter)),
        ((D, 2 * quarter),),
        0,
    )
    mark(pair_w)
    x_block = arrive(dealt).reshape(ROWS, block)
    x_came = over_col(x_block)
    heads = query_weight.shape[1] // 2
    query_weight, key_weight, value_weight, output_weight = ordered_after(
        query_weight, key_weight, value_weight, output_weight
    )
    plan = [
        (kind, False, 0, at, 3 * at + 128 * kind, 128)
        for kind in range(3)
        for at in range(0, heads, 128)
    ]
    qkv_w, out_w = swap_weights(
        (query_weight, key_weight, value_weight, output_weight),
        tuple(plan) + ((3, True, 1, 0, 0, heads),),
        ((D, 3 * heads), (heads, D)),
        1,
    )
    mark(qkv_w)
    top_half = ordered(top_block, arrive(top_col), col)
    top_half = mark(lax.optimization_barrier(top_half))
    x_half = ordered(x_block, arrive(x_came), col)
    x_half = mark(lax.optimization_barrier(x_half))
    top_came = over_x(top_half)
    top_row = over_row(top_half)

    x_other = arrive(over_row(x_half))
    x_full = jnp.concatenate([x_half, x_other], axis=1).astype(F32)
    inverse_first = lax.rsqrt(jnp.mean(x_full * x_full, axis=1, keepdims=True) + EPSILON)
    normed_first = (x_full * inverse_first * gains_full[0][None, :]).astype(BF16)
    normed_first = mark(lax.optimization_barrier(normed_first))
    qkv = multiply(normed_first, qkv_w, False, 384, F32)
    mixed, turned = attend_forward(own_lengths, qkv, tables)
    kept, sent = split_product([mixed], out_w, False, 512)
    mark(sent)
    came = arrive(over_row(sent))
    summed = (kept + came.astype(F32)).astype(BF16)
    summed = mark(lax.optimization_barrier(summed))
    summed_other = over_col(summed)
    top_row = arrive(top_row)
    narrow = half // groups
    first_mine, first_theirs = x_parts(normed_first[:, :half], narrow)
    top_full = jnp.concatenate([top_half, top_row], axis=1)
    (down_w,) = swap_weights(
        (ordered_after(down_weight),),
        ((0, True, 0, 0, 0, down_weight.shape[0] // 2),),
        ((down_weight.shape[0] // 2, D),),
        2,
    )
    hidden_grad = mark(multiply(top_full, down_w, True, 512, F32))
    mixed_mine, mixed_theirs = x_parts(mixed, 2 * mixed.shape[1] // groups)
    top_came = arrive(top_came)
    first_came = over_x(ordered_after(first_theirs))
    summed_other = arrive(summed_other)
    middle = x_half.astype(F32) + (summed.astype(F32) + summed_other.astype(F32))

    middle_low = middle.astype(BF16)
    middle_low, middle = lax.optimization_barrier((middle_low, middle))
    mark(middle_low)
    middle_other = arrive(over_row(middle_low))
    middle_full = jnp.concatenate([middle_low, middle_other], axis=1).astype(F32)
    inverse_second = lax.rsqrt(
        jnp.mean(middle_full * middle_full, axis=1, keepdims=True) + EPSILON
    )
    normed_second = (middle_full * inverse_second * gains_full[1][None, :]).astype(BF16)
    normed_second = mark(lax.optimization_barrier(normed_second))
    hidden, gate_grad, up_grad = feed_forward(normed_second, pair_w, hidden_grad)
    mark(hidden)
    first_came = arrive(first_came)

    def own_block(v):
        return lax.dynamic_slice_in_dim(v, col * block, block, 1)

    def joined(kept, came):
        return mark(lax.optimization_barrier(kept + arrive(came).astype(F32)))

    def to_col(summed):
        theirs = lax.dynamic_slice_in_dim(summed, (1 - col) * block, block, 1)
        return over_col(theirs.astype(BF16))

    second_mine, second_theirs = x_parts(normed_second[:, :half], narrow)
    hidden_mine, hidden_theirs = x_parts(hidden, 2 * quarter // groups)
    hidden_mine, hidden_theirs = lax.optimization_barrier((hidden_mine, hidden_theirs))
    mark(hidden_theirs)

    hidden_came = over_x(hidden_theirs)
    hidden_row = over_row(hidden_mine)
    gate_first, up_first = ordered_after(gate_grad, up_grad)
    kept, sent = split_product([gate_first, up_first], pair_w, True, 512, BUSY)
    mark(sent)
    summed = joined(kept, over_row(sent)).astype(BF16)
    summed_other = over_col(summed)
    gate_row, up_row = over_row(gate_first), over_row(up_first)
    layer_kept, sent = split_product([ordered_after(hidden)], down_w, False, 512)
    mark(sent)
    layer_came = over_row(sent)

    hidden_came, hidden_row = arrive(hidden_came, hidden_row)
    gate_came = over_x(ordered_after(gate_grad))
    hidden_came_row = arrive(over_row(hidden_came))
    down_grads = mark(
        side_grads(
            (hidden_mine, hidden_came), (hidden_row, hidden_came_row), (top_half, top_came)
        )
    )
    down_line = Line(down_grads, side_index)
    down_line.advance()
    mixed_mine, mixed_theirs = x_parts(mixed, 2 * mixed.shape[1] // groups)
    second_came = over_x(ordered_after(second_theirs))
    mixed_came = over_x(ordered_after(mixed_theirs))
    mixed_row = over_row(mixed_mine)

    summed_other = arrive(summed_other)
    second_grad = summed.astype(F32) + summed_other.astype(F32)
    feed_piece = jnp.sum(second_grad * middle * inverse_second, axis=0)
    scaled = second_grad * gains_half[1][None, :]
    dot = jnp.sum(scaled * middle, axis=1, keepdims=True)
    dot = dot + over_row(dot)
    middle_grad = (
        top_half.astype(F32) + scaled * inverse_second - middle * (inverse_second**3 * dot / D)
    )
    branch = middle_grad.astype(BF16)
    middle_grad, branch = lax.optimization_barrier((middle_grad, branch))
    mark(branch)
    branch_row = over_row(branch)
    branch_row = arrive(branch_row)
    branch_full = jnp.concatenate([branch, branch_row], axis=1)
    mixed_grad = mark(multiply(branch_full, out_w, True, 256, BF16))
    down_line.advance()
    dqkv = mark(attend_backward(own_lengths, turned, ordered_after(mixed_grad), tables))
    dqkv_row = over_row(dqkv)
    gate_came, second_came = arrive(gate_came, second_came)
    gate_came_row = over_row(gate_came)
    kept, sent = split_product([ordered_after(dqkv)], qkv_w, True, 512)
    mark(sent)
    came = over_row(sent)
    down_line.advance()
    gate_row, up_row = arrive(gate_row, up_row)
    gate_came_row = arrive(gate_came_row)
    gate_grads = mark(
        wide_grads(
            (second_mine, second_came), (gate_grad, gate_came), (gate_row, gate_came_row)
        )
    )
    mixed_row, mixed_came = arrive(mixed_row, mixed_came)
    mixed_came_row = over_row(mixed_came)
    summed = joined(kept, came)
    first_kept, first_sent = own_block(summed), to_col(summed)
    summed = joined(layer_kept, layer_came)
    layer_kept, layer_sent = own_block(summed), to_col(summed)
    mixed_came_row, dqkv_row = arrive(mixed_came_row, dqkv_row)
    (down_sum,) = down_line.total(1, 1, 4)

    gate_sum, up_sum, qkv_sum, output_sum = tail_sums(
        line,
        3,
        *ordered_after(
            gate_grads,
            up_grad,
            up_row,
            second_mine,
            second_came,
            dqkv,
            dqkv_row,
            first_mine,
            first_came,
            branch,
            mixed_mine,
            mixed_came,
            mixed_row,
            mixed_came_row,
        ),
    )
    mark(output_sum)
    gate_sum = ordered(gate_sum[:, :quarter], gate_sum[:, quarter:], row)
    up_sum = ordered(up_sum[:, :quarter], up_sum[:, quarter:], row)
    qkv_sum = ordered(qkv_sum[:, : 3 * heads], qkv_sum[:, 3 * heads :], row)
    qkv_sums = [
        jnp.concatenate(
            [qkv_sum[:, s : s + 128] for s in range(128 * kind, 6 * heads, 384)], axis=1
        )
        for kind in range(3)
    ]

    first_grad = first_kept + arrive(first_sent).astype(F32)
    x_own = x_block.astype(F32)
    gain_own = own_block(gains_half)
    attention_piece = jnp.sum(first_grad * x_own * inverse_first, axis=0)
    scaled = first_grad * gain_own[0][None, :]
    dot = jnp.sum(scaled * x_own, axis=1, keepdims=True)
    dot = dot + over_row(dot)
    dot = dot + over_col(dot)
    input_grad = (
        own_block(middle_grad) + scaled * inverse_first - x_own * (inverse_first**3 * dot / D)
    ).astype(BF16)
    input_grad = mark(lax.optimization_barrier(input_grad))
    layer_block = own_block(middle) + layer_kept + arrive(layer_sent).astype(F32)
    layer_block = mark(lax.optimization_barrier(layer_block.astype(BF16)))

    gain_sums = all_sum(jnp.stack([attention_piece, own_block(feed_piece[None])[0]]))
    gain_size = block // groups
    gain_sums = lax.dynamic_slice_in_dim(gain_sums, dp * gain_size, gain_size, 1)

    slot_of = jnp.argsort(deal_order, axis=1)[:, :, None, None]

    def returned(v):
        back = lax.all_to_all(
            v.reshape(MICRO, 1, SL, block), "dp", split_axis=2, concat_axis=1, tiled=True
        )
        return jnp.take_along_axis(back, slot_of, axis=1)

    return (
        returned(layer_block),
        returned(input_grad),
        gain_sums[0],
        qkv_sums[0],
        qkv_sums[1],
        qkv_sums[2],
        output_sum,
        gain_sums[1],
        gate_sum,
        up_sum,
        down_sum,
    )


def solution(mesh):
    in_specs = (
        P(None, None, "dp", ("row", "col")),
        P(),
        P(),
        P(("row", "col")),
        P("row", "col"),
        P("row", "col"),
        P("row", "col"),
        P("col", "row"),
        P(("row", "col")),
        P("row", "col"),
        P("row", "col"),
        P("col", "row"),
        P(None, "dp", None, ("row", "col")),
    )
    out_specs = (
        P(None, None, "dp", ("row", "col")),
        P(None, None, "dp", ("row", "col")),
        P(("row", "col", "dp")),
        P(("row", "dp"), "col"),
        P(("row", "dp"), "col"),
        P(("row", "dp"), "col"),
        P(("col", "dp"), "row"),
        P(("row", "col", "dp")),
        P(("row", "dp"), "col"),
        P(("row", "dp"), "col"),
        P(("col", "dp"), "row"),
    )
    return jax.shard_map(
        per_device, mesh=mesh, in_specs=in_specs, out_specs=out_specs, check_vma=False
    )
```

time: 759 us -> 630 us (0.83)
  the two profiles are of different devices: /device:TPU:8 before, /device:TPU:0 now
where the time goes in v2:
time: 630 us; the launch traced here: 619 us
  Pallas kernels  372 us (59%)
  waiting for transfers between devices  87.6 us (14%)
  starting transfers between devices  72.1 us (11%)
  other arithmetic  52.2 us (8%)
  local copies, waits for them, and re-layouts  33.8 us (5%)
    pallas_call x1, Pallas kernels, tail_sums(): pl.pallas_call(lambda *refs: tail_kernel(line, *refs), out_shape=[jax.Sha...  213 us
    pallas_call x4, Pallas kernels, split_product(): pl.pallas_call(kernel, out_shape=(jax.ShapeDtypeStruct((height, width //...  37.4 us
    ppermute x8, waiting for transfers between devices, over_col(): return lax.ppermute(v, 'col', SWAP)  29.6 us
    pallas_call x3, Pallas kernels, swap_weights(): pl.pallas_call(lambda *refs: swap_kernel(plan, len(weights), len(shapes),...  29.1 us
    ppermute x3, starting transfers between devices, advance(): self.right = lax.ppermute(send_right, 'dp', rights)  26.1 us
    pallas_call x3, Pallas kernels, multiply(): pl.pallas_call(kernel, out_shape=jax.ShapeDtypeStruct((height, width), dt...  21.9 us
    ppermute x6, waiting for transfers between devices, over_x(): return lax.ppermute(v, 'dp', [(i, i ^ 1) for i in range(groups)])  19.3 us
    pallas_call x1, Pallas kernels, feed_forward(): pl.pallas_call(feed_kernel, out_shape=(jax.ShapeDtypeStruct((height, widt...  17.1 us
  transfers between devices with their start and end apart: 45, of which 21 were waited for; matrix products, arithmetic and copies ran while one was open for 9% of the time, Pallas kernels for 51%

profile of v2, /device:TPU:0, one launch (start us, length us, event | category | flops | bytes accessed | tf_op | source)
XLA Modules:
  0.0 619.4 jit_solution(16829532373231674742)
XLA Ops:
  6.7 7.3 %all-to-all-start = ((bf16[2,8,32,512]{3,2,0,1:T(8,128)(2,1)}), bf16[2,8,32,512]{3,2,0,1:T(8,128)(2,1)S(1)}, u32[]{:S(2)}, u32[]{:S(2)}) async-start(bf16[2,8,32,512]{3,2,0,1:T(8,128)(2,1)} %copy.41), calls=%async_computation | async-start | bytes 1048576 | tf_op jit(solution)/shard_map/all_to_all | solution.py:871
  17.2 13.6 %shard_map.212.gate_ref.up_ref.refs_2_.refs_3_ = bf16[2048,4096]{1,0:T(8,128)(2,1)} custom-call(bf16[1024,4096]{1,0:T(8,128)(2,1)} %refs_0_, bf16[1024,4096]{1,0:T(8,128)(2,1)} %refs_1_), custom_call_target="tpu_custom_call" | custom-call | tf_op jit(solution)/shard_map/pallas_call | solution.py:447
  31.5 8.0 %shard_map.213 = (bf16[2048,1536]{1,0:T(8,128)(2,1)}, bf16[512,2048]{1,0:T(8,128)(2,1)}) custom-call(bf16[1024,1024]{1,0:T(8,128)(2,1)} %refs_0_.1, bf16[1024,1024]{1,0:T(8,128)(2,1)} %refs_1_.1, bf16[1024,1024]{1,0:T(8,128)(2,1)} %refs_2_, bf16[1024,1024]{1,0:T(8,128)(2,1)} %refs_3_), custom_call_target="tpu_custom_call" | custom-call | tf_op jit(solution)/shard_map/pallas_call | solution.py:447
  39.8 5.2 collective-permute-done
  54.0 8.6 %shard_map.214.qkv_ref = f32[512,1536]{1,0:T(8,128)} custom-call(bf16[512,2048]{1,0:T(8,128)(2,1)} %fusion.2.a_ref, bf16[2048,1536]{1,0:T(8,128)(2,1)} %get-tuple-element.114.w_ref.refs_1_), custom_call_target="tpu_custom_call" | custom-call | tf_op jit(solution)/shard_map/pallas_call | solution.py:186
  62.6 8.9 %shard_map.215 = (bf16[512,512]{1,0:T(8,128)(2,1)}, bf16[512,1536]{1,0:T(8,128)(2,1)}) custom-call(s32[2]{0:T(128)} %copy-done.46, f32[512,1536]{1,0:T(8,128)} %shard_map.214.qkv_ref, f32[256,128]{1,0:T(8,128)} %get-tuple-element.288.cos_ref, f32[256,128]{1,0:T(8,128)} %get-tuple-element.275.first_ref, f32[256,128]{1,0:T(8,128)} %get-tuple-element.274.second_ref), custom_call_target="tpu_custom_call" | custom-call | tf_op jit(solution)/shard_map/pallas_call | solution.py:143
  71.6 5.2 shard_map.216
  83.3 7.5 %shard_map.217.w_ref.refs_1_ = bf16[2048,2048]{1,0:T(8,128)(2,1)} custom-call(bf16[4096,1024]{1,0:T(8,128)(2,1)} %refs_0_.2), custom_call_target="tpu_custom_call" | custom-call | tf_op jit(solution)/shard_map/pallas_call | solution.py:447
  93.6 9.2 %shard_map.218.da_ref = f32[512,2048]{1,0:T(8,128)} custom-call(bf16[512,2048]{1,0:T(8,128)(2,1)} %pad_maximum_fusion.1.a_ref, bf16[2048,2048]{1,0:T(8,128)(2,1)} %shard_map.217.w_ref.refs_1_), custom_call_target="tpu_custom_call" | custom-call | tf_op jit(solution)/shard_map/pallas_call | solution.py:186
  119.3 17.1 %shard_map.219 = (bf16[512,2048]{1,0:T(8,128)(2,1)}, bf16[512,2048]{1,0:T(8,128)(2,1)}, bf16[512,2048]{1,0:T(8,128)(2,1)}) custom-call(bf16[512,2048]{1,0:T(8,128)(2,1)} %fusion.5.x_ref, bf16[2048,4096]{1,0:T(8,128)(2,1)} %shard_map.212.gate_ref.up_ref.refs_2_.refs_3_, bf16[2048,4096]{1,0:T(8,128)(2,1)} %shard_map.212.gate_ref.up_ref.refs_2_.refs_3_, ...), custom_call_target="tpu_custom_call" | custom-call | tf_op jit(solution)/shard_map/pallas_call | solution.py:258
  139.9 14.7 %shard_map.220 = (f32[512,1024]{1,0:T(8,128)}, bf16[512,1024]{1,0:T(8,128)(2,1)}) custom-call(bf16[512,2048]{1,0:T(8,128)(2,1)} %get-tuple-element.154.refs_0_.ro, bf16[512,2048]{1,0:T(8,128)(2,1)} %get-tuple-element.182.refs_1_, bf16[2048,4096]{1,0:T(8,128)(2,1)} %shard_map.212.gate_ref.up_ref.refs_2_.refs_3_, ...), custom_call_target="tpu_custom_call" | custom-call | flops 20000000000 | bytes 60000000 | tf_op jit(solution)/shard_map/pallas_call | solution.py:224
  159.4 9.3 %shard_map.221 = (f32[512,1024]{1,0:T(8,128)}, bf16[512,1024]{1,0:T(8,128)(2,1)}) custom-call(bf16[512,2048]{1,0:T(8,128)(2,1)} %get-tuple-element.139.refs_0_, bf16[2048,2048]{1,0:T(8,128)(2,1)} %shard_map.217.w_ref.refs_1_), custom_call_target="tpu_custom_call" | custom-call | tf_op jit(solution)/shard_map/pallas_call | solution.py:224
  168.7 11.9 %collective-permute-done.13.lr = bf16[512,1024]{1,0:T(8,128)(2,1)} collective-permute-done((bf16[512,1024]{1,0:T(8,128)(2,1)}, bf16[512,1024]{1,0:T(8,128)(2,1)}, u32[]{:S(2)}, u32[]{:S(2)}) %collective-permute-start.13) | collective-permute-done | bytes 1048608 | tf_op jit(solution)/shard_map/ppermute | solution.py:779
  183.6 9.1 %shard_map.222.gr_ref.gl_ref.refs_1_ = bf16[2048,1024]{1,0:T(8,128)(2,1)} custom-call(bf16[512,1024]{1,0:T(8,128)(2,1)} %get-tuple-element.143.lo, bf16[512,1024]{1,0:T(8,128)(2,1)} %collective-permute-done.13.lr, bf16[512,1024]{1,0:T(8,128)(2,1)} %collective-permute-done.14.xo, bf16[512,1024]{1,0:T(8,128)(2,1)} %collective-permute-done.15.xr, ...), custom_call_target="tpu_custom_call" | custom-call | tf_op jit(solution)/shard_map/pallas_call | solution.py:288
  192.7 13.6 %collective-permute-done.12 = bf16[512,1024]{1,0:T(8,128)(2,1)} collective-permute-done((bf16[512,1024]{1,0:T(8,128)(2,1)S(1)}, bf16[512,1024]{1,0:T(8,128)(2,1)}, u32[]{:S(2)}, u32[]{:S(2)}) %collective-permute-start.12) | collective-permute-done | bytes 1048608 | tf_op jit(solution)/shard_map/ppermute | solution.py:776
  232.6 10.1 %collective-permute-done.18.r_ref = bf16[512,1024]{1,0:T(8,128)(2,1)S(1)} collective-permute-done((bf16[512,1024]{1,0:T(8,128)(2,1)}, bf16[512,1024]{1,0:T(8,128)(2,1)S(1)}, u32[]{:S(2)}, u32[]{:S(2)}) %collective-permute-start.18) | collective-permute-done | bytes 1048608 | tf_op jit(solution)/shard_map/ppermute | solution.py:842
  248.6 11.0 %shard_map.225.refs_0_.refs_5_ = bf16[512,1536]{1,0:T(8,128)(2,1)} custom-call(s32[2]{0:T(128)} %copy-done.46, bf16[512,1536]{1,0:T(8,128)(2,1)} %get-tuple-element.142.turned_ref, bf16[512,512]{1,0:T(8,128)(2,1)} %shard_map.223.od_ref, f32[256,128]{1,0:T(8,128)} %get-tuple-element.288.cos_ref, f32[256,128]{1,0:T(8,128)} %get-tuple-element.275.first_ref, ...), custom_call_target="tpu_custom_call" | custom-call | tf_op jit(solution)/shard_map/pallas_call | solution.py:161
  264.7 5.4 collective-permute-start.27
  277.0 8.1 %shard_map.226 = (f32[512,1024]{1,0:T(8,128)}, bf16[512,1024]{1,0:T(8,128)(2,1)}) custom-call(bf16[512,1536]{1,0:T(8,128)(2,1)} %shard_map.225.refs_0_.refs_5_, bf16[2048,1536]{1,0:T(8,128)(2,1)} %get-tuple-element.114.w_ref.refs_1_), custom_call_target="tpu_custom_call" | custom-call | tf_op jit(solution)/shard_map/pallas_call | solution.py:224
  285.7 6.6 %collective-permute-done.27.r_ref = bf16[512,1024]{1,0:T(8,128)(2,1)} collective-permute-done((bf16[512,1024]{1,0:T(8,128)(2,1)}, bf16[512,1024]{1,0:T(8,128)(2,1)}, u32[]{:S(2)}, u32[]{:S(2)}) %collective-permute-start.27) | collective-permute-done | bytes 1048608 | tf_op jit(solution)/shard_map/ppermute | solution.py:842
  301.2 16.9 %collective-permute-start.35 = (bf16[512,1024]{1,0:T(8,128)(2,1)}, bf16[512,1024]{1,0:T(8,128)(2,1)}, u32[]{:S(2)}, u32[]{:S(2)}) collective-permute-start(bf16[512,1024]{1,0:T(8,128)(2,1)} %get-tuple-element.178), channel_id=1, source_target_pairs={{0,8},{4,12},{8,16},{12,20},{16,24},{20,28},{1,9},{5,13},{9,17},{1... | collective-permute-start | bytes 3145736 | tf_op jit(solution)/shard_map/ppermute | solution.py:842
  320.6 9.7 %shard_map.228.refs_0_ = bf16[512,4096]{1,0:T(8,128)(2,1)} custom-call(bf16[512,512]{1,0:T(8,128)(2,1)} %get-tuple-element.184.lo.refs_3_, bf16[512,512]{1,0:T(8,128)(2,1)} %copy-done.21, bf16[512,2048]{1,0:T(8,128)(2,1)} %get-tuple-element.154.refs_0_.ro, bf16[512,2048]{1,0:T(8,128)(2,1)} %collective-permute-done.20.rr, ...), custom_call_target="tpu_custom_call" | custom-call | tf_op jit(solution)/shard_map/pallas_call | solution.py:314
  348.0 212.9 %shard_map.230 = (f32[128,4096]{1,0:T(8,128)}, f32[128,4096]{1,0:T(8,128)}, f32[128,3072]{1,0:T(8,128)}, f32[128,1024]{1,0:T(8,128)}) custom-call(bf16[512,4096]{1,0:T(8,128)(2,1)} %shard_map.228.refs_0_, bf16[512,2048]{1,0:T(8,128)(2,1)} %get-tuple-element.182.refs_1_, bf16[512,2048]{1,0:T(8,128)(2,1)} %collective-permute-done.26.refs_2_, ...), custom_call_target="tpu_custom_call" | custom-call | tf_op jit(solution)/shard_map/pallas_call | solution.py:727
  607.0 8.0 %collective-permute-done.41 = f32[2,512]{1,0:T(2,128)S(1)} collective-permute-done((f32[2,512]{1,0:T(2,128)S(1)}, f32[2,512]{1,0:T(2,128)S(1)}, u32[]{:S(2)}, u32[]{:S(2)}) %collective-permute-start.41) | collective-permute-done | bytes 4128 | tf_op jit(solution)/shard_map/ppermute | solution.py:865
  (278 shorter events, 179.5 us)
Async XLA Ops:
  6.7 24.1 %all-to-all-start = ((bf16[2,8,32,512]{3,2,0,1:T(8,128)(2,1)}), bf16[2,8,32,512]{3,2,0,1:T(8,128)(2,1)S(1)}, u32[]{:S(2)}, u32[]{:S(2)}) async-start(bf16[2,8,32,512]{3,2,0,1:T(8,128)(2,1)} %copy.41), calls=%async_computation | async-start | bytes 1048576 | tf_op jit(solution)/shard_map/all_to_all | solution.py:871
  15.7 23.8 %collective-permute-start.1 = (bf16[512,512]{1,0:T(8,128)(2,1)S(1)}, bf16[512,512]{1,0:T(8,128)(2,1)S(1)}, u32[]{:S(2)}, u32[]{:S(2)}) collective-permute-start(bf16[512,512]{1,0:T(8,128)(2,1)S(1)} %bitcast_select_fusion), channel_id=1, source_target_pairs={{0,1},{1,0},{2,3},{3,2},{4,5},{5,4},{6,7},{7,6},{8,9},{9,8},{10,11... | collective-permute-start | bytes 1572872 | tf_op jit(solution)/shard_map/ppermute | solution.py:776
  77.3 25.9 %collective-permute-start.7 = (bf16[512,1024]{1,0:T(8,128)(2,1)S(1)}, bf16[512,1024]{1,0:T(8,128)(2,1)}, u32[]{:S(2)}, u32[]{:S(2)}) collective-permute-start(bf16[512,1024]{1,0:T(8,128)(2,1)S(1)} %maximum_select_fusion.3.ro), channel_id=1, source_target_pairs={{0,4},{4,0},{8,12},{12,8},{16,20},{20,16},{24,28},{28,24},{1,5},{5... | collective-permute-start | bytes 3145736 | tf_op jit(solution)/shard_map/ppermute | solution.py:779
  82.8 25.6 %collective-permute-start.6 = (bf16[512,1024]{1,0:T(8,128)(2,1)S(1)}, bf16[512,1024]{1,0:T(8,128)(2,1)}, u32[]{:S(2)}, u32[]{:S(2)}) collective-permute-start(bf16[512,1024]{1,0:T(8,128)(2,1)S(1)} %add_convert_fusion), channel_id=1, source_target_pairs={{0,1},{1,0},{2,3},{3,2},{4,5},{5,4},{6,7},{7,6},{8,9},{9,8},{10,11... | collective-permute-start | bytes 3145736 | tf_op jit(solution)/shard_map/ppermute | solution.py:776
  154.7 25.9 %collective-permute-start.13 = (bf16[512,1024]{1,0:T(8,128)(2,1)}, bf16[512,1024]{1,0:T(8,128)(2,1)}, u32[]{:S(2)}, u32[]{:S(2)}) collective-permute-start(bf16[512,1024]{1,0:T(8,128)(2,1)} %get-tuple-element.133), channel_id=1, source_target_pairs={{0,4},{4,0},{8,12},{12,8},{16,20},{20,16},{24,28},{28,24},{1,5},{5... | collective-permute-start | bytes 3145736 | tf_op jit(solution)/shard_map/ppermute | solution.py:779
  156.6 24.0 %collective-permute-start.14 = (bf16[512,1024]{1,0:T(8,128)(2,1)}, bf16[512,1024]{1,0:T(8,128)(2,1)}, u32[]{:S(2)}, u32[]{:S(2)}) collective-permute-start(bf16[512,1024]{1,0:T(8,128)(2,1)} %get-tuple-element.143.lo), channel_id=1, source_target_pairs={{0,2},{2,0},{1,3},{3,1},{4,6},{6,4},{5,7},{7,5},{8,10},{10,8},{9,1... | collective-permute-start | bytes 3145736 | tf_op jit(solution)/shard_map/ppermute | solution.py:773
  180.6 25.7 %collective-permute-start.12 = (bf16[512,1024]{1,0:T(8,128)(2,1)S(1)}, bf16[512,1024]{1,0:T(8,128)(2,1)}, u32[]{:S(2)}, u32[]{:S(2)}) collective-permute-start(bf16[512,1024]{1,0:T(8,128)(2,1)S(1)} %convert_add_fusion.3), channel_id=1, source_target_pairs={{0,1},{1,0},{2,3},{3,2},{4,5},{5,4},{6,7},{7,6},{8,9},{9,8},{10,11... | collective-permute-start | bytes 3145736 | tf_op jit(solution)/shard_map/ppermute | solution.py:776
  181.2 78.4 %collective-permute-start.20 = (bf16[512,2048]{1,0:T(8,128)(2,1)}, bf16[512,2048]{1,0:T(8,128)(2,1)}, u32[]{:S(2)}, u32[]{:S(2)}) collective-permute-start(bf16[512,2048]{1,0:T(8,128)(2,1)} %get-tuple-element.154.refs_0_.ro), channel_id=1, source_target_pairs={{0,4},{4,0},{8,12},{12,8},{16,20},{20,16},{24,28},{28,24},{1,5},{5... | collective-permute-start | bytes 6291464 | tf_op jit(solution)/shard_map/ppermute | solution.py:779
  215.7 26.9 %collective-permute-start.18 = (bf16[512,1024]{1,0:T(8,128)(2,1)}, bf16[512,1024]{1,0:T(8,128)(2,1)S(1)}, u32[]{:S(2)}, u32[]{:S(2)}) collective-permute-start(bf16[512,1024]{1,0:T(8,128)(2,1)} %get-tuple-element.211), channel_id=1, source_target_pairs={{0,8},{4,12},{1,9},{5,13},{2,10},{6,14},{3,11},{7,15}} | collective-permute-start | bytes 3145736 | tf_op jit(solution)/shard_map/ppermute | solution.py:842
  220.2 65.0 %collective-permute-start.25 = (bf16[512,2048]{1,0:T(8,128)(2,1)}, bf16[512,2048]{1,0:T(8,128)(2,1)}, u32[]{:S(2)}, u32[]{:S(2)}) collective-permute-start(bf16[512,2048]{1,0:T(8,128)(2,1)} %get-tuple-element.154.refs_0_.ro), channel_id=1, source_target_pairs={{0,2},{2,0},{1,3},{3,1},{4,6},{6,4},{5,7},{7,5},{8,10},{10,8},{9,1... | collective-permute-start | bytes 6291464 | tf_op jit(solution)/shard_map/ppermute | solution.py:773
  222.9 62.3 %collective-permute-start.26 = (bf16[512,2048]{1,0:T(8,128)(2,1)}, bf16[512,2048]{1,0:T(8,128)(2,1)}, u32[]{:S(2)}, u32[]{:S(2)}) collective-permute-start(bf16[512,2048]{1,0:T(8,128)(2,1)} %get-tuple-element.182.refs_1_), channel_id=1, source_target_pairs={{0,2},{2,0},{1,3},{3,1},{4,6},{6,4},{5,7},{7,5},{8,10},{10,8},{9,1... | collective-permute-start | bytes 6291464 | tf_op jit(solution)/shard_map/ppermute | solution.py:773
  223.4 36.2 %collective-permute-start.21 = (bf16[512,512]{1,0:T(8,128)(2,1)S(1)}, bf16[512,512]{1,0:T(8,128)(2,1)S(1)}, u32[]{:S(2)}, u32[]{:S(2)}) collective-permute-start(bf16[512,512]{1,0:T(8,128)(2,1)S(1)} %get-tuple-element.155), channel_id=1, source_target_pairs={{0,4},{4,0},{8,12},{12,8},{16,20},{20,16},{24,28},{28,24},{1,5},{5... | collective-permute-start | bytes 1572872 | tf_op jit(solution)/shard_map/ppermute | solution.py:779
  259.6 58.5 %collective-permute-start.29 = (bf16[512,2048]{1,0:T(8,128)(2,1)}, bf16[512,2048]{1,0:T(8,128)(2,1)}, u32[]{:S(2)}, u32[]{:S(2)}) collective-permute-start(bf16[512,2048]{1,0:T(8,128)(2,1)} %collective-permute-done.20.rr), channel_id=1, source_target_pairs={{0,2},{2,0},{1,3},{3,1},{4,6},{6,4},{5,7},{7,5},{8,10},{10,8},{9,1... | collective-permute-start | bytes 6291464 | tf_op jit(solution)/shard_map/ppermute | solution.py:773
  264.7 27.5 %collective-permute-start.27 = (bf16[512,1024]{1,0:T(8,128)(2,1)}, bf16[512,1024]{1,0:T(8,128)(2,1)}, u32[]{:S(2)}, u32[]{:S(2)}) collective-permute-start(bf16[512,1024]{1,0:T(8,128)(2,1)} %get-tuple-element.162), channel_id=1, source_target_pairs={{0,8},{4,12},{8,16},{12,20},{1,9},{5,13},{9,17},{13,21},{2,10},{6,... | collective-permute-start | bytes 3145736 | tf_op jit(solution)/shard_map/ppermute | solution.py:842
  275.4 16.9 %collective-permute-start.28 = (bf16[512,1024]{1,0:T(8,128)(2,1)}, bf16[512,1024]{1,0:T(8,128)(2,1)}, u32[]{:S(2)}, u32[]{:S(2)}) collective-permute-start(bf16[512,1024]{1,0:T(8,128)(2,1)} %get-tuple-element.152), channel_id=1, source_target_pairs={{28,20},{24,16},{20,12},{16,8},{29,21},{25,17},{21,13},{17,9},{30,... | collective-permute-start | bytes 3145736 | tf_op jit(solution)/shard_map/ppermute | solution.py:843
  285.2 45.2 %collective-permute-start.22 = (bf16[512,1024]{1,0:T(8,128)(2,1)}, bf16[512,1024]{1,0:T(8,128)(2,1)}, u32[]{:S(2)}, u32[]{:S(2)}) collective-permute-start(bf16[512,1024]{1,0:T(8,128)(2,1)} %get-tuple-element.159), channel_id=1, source_target_pairs={{0,2},{2,0},{1,3},{3,1},{4,6},{6,4},{5,7},{7,5},{8,10},{10,8},{9,1... | collective-permute-start | bytes 3145736 | tf_op jit(solution)/shard_map/ppermute | solution.py:773
  285.2 47.5 %collective-permute-start.11 = (bf16[512,1024]{1,0:T(8,128)(2,1)}, bf16[512,1024]{1,0:T(8,128)(2,1)}, u32[]{:S(2)}, u32[]{:S(2)}) collective-permute-start(bf16[512,1024]{1,0:T(8,128)(2,1)} %get-tuple-element.141), channel_id=1, source_target_pairs={{0,2},{2,0},{1,3},{3,1},{4,6},{6,4},{5,7},{7,5},{8,10},{10,8},{9,1... | collective-permute-start | bytes 3145736 | tf_op jit(solution)/shard_map/ppermute | solution.py:773
  292.2 45.3 %collective-permute-start.33 = (bf16[512,1536]{1,0:T(8,128)(2,1)S(1)}, bf16[512,1536]{1,0:T(8,128)(2,1)S(1)}, u32[]{:S(2)}, u32[]{:S(2)}) collective-permute-start(bf16[512,1536]{1,0:T(8,128)(2,1)S(1)} %copy-done.6), channel_id=1, source_target_pairs={{0,2},{2,0},{1,3},{3,1},{4,6},{6,4},{5,7},{7,5},{8,10},{10,8},{9,1... | collective-permute-start | bytes 4718600 | tf_op jit(solution)/shard_map/ppermute | solution.py:773
  301.2 38.6 %collective-permute-start.35 = (bf16[512,1024]{1,0:T(8,128)(2,1)}, bf16[512,1024]{1,0:T(8,128)(2,1)}, u32[]{:S(2)}, u32[]{:S(2)}) collective-permute-start(bf16[512,1024]{1,0:T(8,128)(2,1)} %get-tuple-element.178), channel_id=1, source_target_pairs={{0,8},{4,12},{8,16},{12,20},{16,24},{20,28},{1,9},{5,13},{9,17},{1... | collective-permute-start | bytes 3145736 | tf_op jit(solution)/shard_map/ppermute | solution.py:842
  318.1 25.1 %collective-permute-start.36 = (bf16[512,1024]{1,0:T(8,128)(2,1)}, bf16[512,1024]{1,0:T(8,128)(2,1)}, u32[]{:S(2)}, u32[]{:S(2)}) collective-permute-start(bf16[512,1024]{1,0:T(8,128)(2,1)} %get-tuple-element.165), channel_id=1, source_target_pairs={{28,20},{24,16},{20,12},{16,8},{12,4},{8,0},{29,21},{25,17},{21,13... | collective-permute-start | bytes 3145736 | tf_op jit(solution)/shard_map/ppermute | solution.py:843
  336.1 232.4 %collective-permute-start.31 = (bf16[512,512]{1,0:T(8,128)(2,1)}, bf16[512,512]{1,0:T(8,128)(2,1)}, u32[]{:S(2)}, u32[]{:S(2)}) collective-permute-start(bf16[512,512]{1,0:T(8,128)(2,1)} %dynamic-slice_convert_fusion), channel_id=1, source_target_pairs={{0,1},{1,0},{2,3},{3,2},{4,5},{5,4},{6,7},{7,6},{8,9},{9,8},{10,11... | collective-permute-start | bytes 1572872 | tf_op jit(solution)/shard_map/ppermute | solution.py:776
  337.6 254.4 %collective-permute-start.30 = (bf16[512,512]{1,0:T(8,128)(2,1)}, bf16[512,512]{1,0:T(8,128)(2,1)}, u32[]{:S(2)}, u32[]{:S(2)}) collective-permute-start(bf16[512,512]{1,0:T(8,128)(2,1)} %dynamic-slice_convert_fusion.1), channel_id=1, source_target_pairs={{0,1},{1,0},{2,3},{3,2},{4,5},{5,4},{6,7},{7,6},{8,9},{9,8},{10,11... | collective-permute-start | bytes 1572872 | tf_op jit(solution)/shard_map/ppermute | solution.py:776
  579.6 17.6 %all-to-all-start.2 = ((bf16[2,1,256,512]{3,0,1,2:T(2,128)(2,1)}), bf16[2,1,256,512]{3,0,1,2:T(2,128)(2,1)S(1)}, u32[]{:S(2)}, u32[]{:S(2)}) async-start(bf16[2,1,256,512]{3,0,1,2:T(2,128)(2,1)} %copy.47), calls=%async_computation.2 | async-start | bytes 1048576 | tf_op jit(solution)/shard_map/all_to_all | solution.py:1098
  597.2 19.1 %all-to-all-start.1 = ((bf16[2,1,256,512]{3,0,1,2:T(2,128)(2,1)}), bf16[2,1,256,512]{3,0,1,2:T(2,128)(2,1)S(1)}, u32[]{:S(2)}, u32[]{:S(2)}) async-start(bf16[2,1,256,512]{3,0,1,2:T(2,128)(2,1)} %copy.45), calls=%async_computation.1 | async-start | bytes 1048576 | tf_op jit(solution)/shard_map/all_to_all | solution.py:1098
  (69 other events, 637.8 us)
